TPU v7x, 512 devices: a whole 4x8x8 slice. The times are simulated.
512 devices in a mesh: expert: 128 (over y, z, core), dp: 4 (over x).
Axes of the slice: x: 4, y: 8, z: 8, core: 2. Of those that a mesh axis runs over, the one named last changes fastest.
Arguments:
- hidden: bfloat16 [128, 4, 256, 1024], P('expert', 'dp'), may hold values from -6 to 6
- w_down: bfloat16 [128, 1024, 3584], P('expert', 'dp'), may hold values from -0.1875 to 0.1875
- expert_ids: int32 [4, 2048, 8], P('dp', 'expert'), may hold values from 0 to 127, all different within a row; in each aligned block of 16 rows (0 to 15, 16 to 31, ..., all dimensions but the last counted through in order) at most 2 rows name the same one
- route_weights: float32 [4, 2048, 8], P('dp', 'expert'), may hold values from 0.1 to 0.6
- grad_out: bfloat16 [4, 2048, 3584], P('dp', 'expert'), may hold values from -6 to 6
Outputs:
- mixed: bfloat16 [4, 2048, 3584], P('dp', 'expert')
- d_hidden: bfloat16 [128, 4, 256, 1024], P('expert', 'dp')
- d_w_down: bfloat16 [128, 1024, 3584], P('expert', 'dp')
- d_route: float32 [4, 2048, 8], P('dp', 'expert')
Inputs may be any that keep to these rules, and one draw needn't show every extreme that they name: `expert_ids`: among the 16 tokens of one device no expert is chosen more than 2 times, and some expert is chosen exactly 2 times; the 8 choices of a token are distinct.
All inputs are finite; a program needn't handle non-finite values.
Results may differ from a plain program's by a relative error of at most 0.0085.
Values may be sent and summed in bfloat16 or wider, within the bound.
A program may use at most 128 MiB of HBM per device.

v0:
```python
import jax
import jax.numpy as jnp
from jax import lax
from jax.sharding import PartitionSpec as P


def slot_ranks(choices, experts):
    flat = choices.reshape(-1)
    onehot = (flat[:, None] == jnp.arange(experts, dtype=jnp.int32)[None, :]).astype(jnp.int32)
    earlier = jnp.cumsum(onehot, axis=0) - onehot
    return jnp.sum(earlier * onehot, axis=1).reshape(choices.shape)


def on_device(hidden, w_down, expert_ids, route_weights, grad_out):
    experts = lax.axis_size("expert")
    groups = lax.axis_size("dp")
    slots = hidden.shape[2] // experts
    width = w_down.shape[2]
    w_whole = lax.all_gather(w_down, "dp", axis=1, tiled=True)[0]
    out_slots = jnp.dot(hidden[0, 0], w_whole, preferred_element_type=jnp.float32).astype(
        jnp.bfloat16
    )
    arrived = lax.all_to_all(
        out_slots.reshape(experts, slots, width), "expert", split_axis=0, concat_axis=0, tiled=True
    )
    arrived = arrived.reshape(experts * slots, width)
    choices = expert_ids[0]
    weights = route_weights[0]
    cotangent = grad_out[0].astype(jnp.float32)
    rows = choices * slots + slot_ranks(choices, experts)
    out_pair = arrived[rows].astype(jnp.float32)
    mixed = jnp.einsum("tk,tkd->td", weights, out_pair)
    d_route = jnp.einsum("td,tkd->tk", cotangent, out_pair)
    grad_pair = (weights[..., None] * cotangent[:, None, :]).astype(jnp.bfloat16)
    outgoing = jnp.zeros((experts * slots, width), jnp.bfloat16)
    outgoing = outgoing.at[rows.reshape(-1)].set(grad_pair.reshape(-1, width))
    mine = lax.all_to_all(
        outgoing.reshape(experts, 1, slots, width),
        "expert",
        split_axis=0,
        concat_axis=0,
        tiled=True,
    )
    own_grads = mine[:, 0]
    slot_grads = lax.all_gather(mine, "dp", axis=1, tiled=True)
    d_hidden = jnp.einsum(
        "rd,hd->rh", own_grads.reshape(-1, width), w_whole, preferred_element_type=jnp.float32
    ).astype(jnp.bfloat16)
    columns = lax.all_to_all(hidden, "dp", split_axis=3, concat_axis=1, tiled=True)[0]
    columns = columns.reshape(groups, experts, slots, columns.shape[-1])
    d_weight = jnp.einsum(
        "gsch,sgcd->hd", columns, slot_grads, preferred_element_type=jnp.float32
    ).astype(jnp.bfloat16)
    return (
        mixed.astype(jnp.bfloat16)[None],
        d_hidden.reshape(hidden.shape),
        d_weight[None],
        d_route[None],
    )


def solution(mesh):
    placed = (
        P("expert", "dp", None, None),
        P("expert", "dp", None),
        P("dp", "expert", None),
        P("dp", "expert", None),
        P("dp", "expert", None),
    )
    return jax.shard_map(
        on_device,
        mesh=mesh,
        in_specs=placed,
        out_specs=(
            P("dp", "expert", None),
            P("expert", "dp", None, None),
            P("expert", "dp", None),
            P("dp", "expert", None),
        ),
        check_vma=False,
    )
```

profile of v0, /device:TPU:1, one launch (start us, length us, event | category | flops | bytes accessed | tf_op | source)
XLA Modules:
  0.0 197.7 jit_solution(9017277390061045914)
XLA Ops:
  7.2 0.7 all-gather.3.cloned.1.call-update
  8.6 0.2 reduce_window_sum.11
  8.8 0.2 select_reduce_fusion
  9.0 2.5 %scatter_custom_fusion = bf16[256,3584]{1,0:T(8,128)(2,1)S(1)} fusion(s32[128]{0:T(128)S(1)} %fusion.30, f32[16,3584]{1,0:T(8,128)S(1)} %bitcast_convert_fusion.1, f32[128]{0:T(128)S(1)} %mul.53, bf16[]{:T(256)} %constant.7.clone.1), kind=kCustom, calls=%fused_computation.14 | custom fusion | flops 917504 | bytes 2064898 | tf_op jit(solution)/shard_map/scatter | solution.py:36
  11.5 1.6 reshape.99
  13.2 64.9 %all_to_all.25 = bf16[128,1,2,3584]{3,2,1,0:T(2,128)(2,1)S(1)} all-to-all(bf16[128,1,2,3584]{3,2,1,0:T(2,128)(2,1)} %bitcast.75), channel_id=1, replica_groups=mesh['expert'=128,'dp'=4] {'expert'}, dimensions={0} | all-to-all | bytes 3670016 | tf_op jit(solution)/shard_map/all_to_all | solution.py:37
  78.1 3.7 %copy.52 = bf16[128,1,2,3584]{0,3,1,2:T(8,128)(2,1)} copy(bf16[128,1,2,3584]{3,2,1,0:T(2,128)(2,1)S(1)} %all_to_all.25) | data formatting | bytes 3670016 | tf_op jit(solution)/shard_map/all_to_all | solution.py:37
  81.8 1.0 copy-done
  82.8 0.8 copy.53
  83.7 0.5 broadcast.58
  84.2 3.8 %reduce = bf16[1024,256]{1,0:T(8,128)(2,1)S(1)} reduce(bf16[1024,1,1,256]{3,2,1,0:T(2,128)(2,1)S(1)} %bitcast.77, bf16[]{:T(256)} %broadcast.58), dimensions={1,2}, to_apply=%bitcast.68.reduce_sub_computation | reduce | bytes 1048578
  88.0 0.9 reshape.125
  88.9 4.0 %all-to-all-start.2 = ((bf16[4,2,32768]{2,1,0:T(2,128)(2,1)}), bf16[4,2,32768]{2,1,0:T(2,128)(2,1)S(1)}, u32[]{:S(2)}, u32[]{:S(2)}) async-start(bf16[4,2,32768]{2,1,0:T(2,128)(2,1)} %reshape.125), calls=%async_computation.2 | async-start | bytes 1048576 | tf_op jit(solution)/shard_map/all_to_all | solution.py:49
  93.0 2.2 %all-gather.3.cloned.1.call-done = bf16[1,1024,3584]{2,1,0:T(8,128)(2,1)} async-done(((bf16[1,256,3584]{2,1,0:T(8,128)(2,1)}), bf16[1,1024,3584]{2,1,0:T(8,128)(2,1)}) %all-gather.3.cloned.1.call-update) | async-done | bytes 7340048 | tf_op jit(solution)/shard_map/all_gather | solution.py:19
  95.1 6.4 %fusion.5 = bf16[256,3584]{1,0:T(8,128)(2,1)} fusion(bf16[1,1024,3584]{2,1,0:T(8,128)(2,1)} %all-gather.3.cloned.1.call-done, bf16[1,1,256,1024]{3,2,1,0:T(8,128)(2,1)S(1)} %copy-done.1), kind=kOutput, calls=%fused_computation.8 | convolution fusion | flops 1879965696 | bytes 9699328 | tf_op jit(solution)/shard_map/dot_general | solution.py:20
  101.5 4.7 %reshape.96 = bf16[128,2,3584]{2,1,0:T(2,128)(2,1)} reshape(bf16[256,3584]{1,0:T(8,128)(2,1)} %fusion.5) | data formatting | bytes 3670016 | tf_op jit(solution)/shard_map/reshape | solution.py:24
  106.2 20.2 %all-to-all-start = ((bf16[128,2,3584]{2,1,0:T(2,128)(2,1)}), bf16[128,2,3584]{2,1,0:T(2,128)(2,1)}, u32[]{:S(2)}, u32[]{:S(2)}) async-start(bf16[128,2,3584]{2,1,0:T(2,128)(2,1)} %reshape.96), calls=%async_computation | async-start | bytes 3670016 | tf_op jit(solution)/shard_map/all_to_all | solution.py:23
  126.7 0.1 reshape.103
  126.9 0.5 reshape.126
  127.5 0.3 copy.54
  127.8 1.6 reshape_squeeze.6
  129.5 6.6 %fusion.13 = bf16[1,1,256,1024]{3,2,1,0:T(8,128)(2,1)} fusion(bf16[256,3584]{1,0:T(8,128)(2,1)} %reshape_squeeze.6, bf16[1,1024,3584]{2,1,0:T(8,128)(2,1)} %all-gather.3.cloned.1.call-done), kind=kOutput, calls=%fused_computation.13 | convolution fusion | flops 1879310336 | bytes 9699328 | tf_op jit(solution)/shard_map/rd,hd->rh/dot_general | solution.py:46
  136.1 36.5 %all-to-all-done = bf16[128,2,3584]{2,1,0:T(2,128)(2,1)} async-done(((bf16[128,2,3584]{2,1,0:T(2,128)(2,1)}), bf16[128,2,3584]{2,1,0:T(2,128)(2,1)}, u32[]{:S(2)}, u32[]{:S(2)}) %all-to-all-start) | async-done | bytes 1835040 | tf_op jit(solution)/shard_map/all_to_all | solution.py:23
  172.6 4.1 %reshape.97 = bf16[256,3584]{1,0:T(8,128)(2,1)S(1)} reshape(bf16[128,2,3584]{2,1,0:T(2,128)(2,1)} %all-to-all-done) | data formatting | bytes 3670016 | tf_op jit(solution)/shard_map/reshape | solution.py:26
  176.7 1.1 gather_fusion
  177.8 0.4 fusion.18
  178.2 0.7 copy.70
  178.9 0.6 fusion.20
  179.5 0.7 copy.61
  180.2 3.0 %all-gather.5.cloned.1.call-done = bf16[128,4,2,3584]{0,3,1,2:T(8,128)(2,1)} async-done(((bf16[128,1,2,3584]{0,3,1,2:T(8,128)(2,1)}), bf16[128,4,2,3584]{0,3,1,2:T(8,128)(2,1)}) %all-gather.5.cloned.1.call-update) | async-done | bytes 7340048 | tf_op jit(solution)/shard_map/all_gather | solution.py:45
  183.1 5.2 %fusion.8 = bf16[1,256,3584]{1,2,0:T(8,128)(2,1)S(1)} fusion(bf16[128,4,2,3584]{0,3,1,2:T(8,128)(2,1)} %all-gather.5.cloned.1.call-done, bf16[4,128,2,256]{3,0,2,1:T(4,128)(2,1)S(1)} %bitcast.79), kind=kOutput, calls=%fused_computation.9 | convolution fusion | flops 1879965696 | bytes 9699328 | tf_op jit(solution)/shard_map/gsch,sgcd->hd/dot_general | solution.py:51
  188.3 2.6 %copy.56 = bf16[1,256,3584]{2,1,0:T(8,128)(2,1)} copy(bf16[1,256,3584]{1,2,0:T(8,128)(2,1)S(1)} %fusion.8) | data formatting | bytes 3670016
  (30 shorter events, 1.1 us)
Async XLA Ops:
  7.2 0.8 copy-start.3
  7.2 1.1 copy-start.4
  7.2 1.8 copy-start.2
  7.2 87.9 %all-gather.3.cloned.1.call-start = ((), (), s32[]{:S(2)}) async-start(), calls=%async_computation.3 | async-start | bytes 9175040 | tf_op jit(solution)/shard_map/all_gather | solution.py:19
  7.9 175.2 %all-gather.5.cloned.1.call-start = ((), (), s32[]{:S(2)}) async-start(), calls=%async_computation.4 | async-start | bytes 9175040 | tf_op jit(solution)/shard_map/all_gather | solution.py:45
  81.8 1.0 copy-start
  88.0 7.1 %copy-start.1 = (bf16[1,1,256,1024]{3,2,1,0:T(8,128)(2,1)S(1)}, bf16[1,1,256,1024]{3,2,1,0:T(8,128)(2,1)}, u32[]{:S(2)}) copy-start(bf16[1,1,256,1024]{3,2,1,0:T(8,128)(2,1)} %param.5) | copy-start | bytes 1572868
  88.9 17.3 %all-to-all-start.2 = ((bf16[4,2,32768]{2,1,0:T(2,128)(2,1)}), bf16[4,2,32768]{2,1,0:T(2,128)(2,1)S(1)}, u32[]{:S(2)}, u32[]{:S(2)}) async-start(bf16[4,2,32768]{2,1,0:T(2,128)(2,1)} %reshape.125), calls=%async_computation.2 | async-start | bytes 1048576 | tf_op jit(solution)/shard_map/all_to_all | solution.py:49
  106.2 66.4 %all-to-all-start = ((bf16[128,2,3584]{2,1,0:T(2,128)(2,1)}), bf16[128,2,3584]{2,1,0:T(2,128)(2,1)}, u32[]{:S(2)}, u32[]{:S(2)}) async-start(bf16[128,2,3584]{2,1,0:T(2,128)(2,1)} %reshape.96), calls=%async_computation | async-start | bytes 3670016 | tf_op jit(solution)/shard_map/all_to_all | solution.py:23
Sparse Core Ops, SparseCore 0:
  10.1 84.9 all-gather.2
  97.2 85.8 all-gather.4
where the time goes:
time: 198 us
  blocking collectives  64.9 us (33%)
  waiting for transfers between devices  42.3 us (21%)
  local copies, waits for them, and re-layouts  25.9 us (13%)
  starting transfers between devices  24.3 us (12%)
  matrix products  19.2 us (10%)
  between operations  14.2 us (7%)
  other arithmetic  6.83 us (3%)
    all_to_all x1, blocking collectives, on_device(): lax.all_to_all(outgoing.reshape(experts, 1, slots, width), 'expert', spli...  64.9 us
    all_to_all x1, waiting for transfers between devices, on_device(): lax.all_to_all(out_slots.reshape(experts, slots, width), 'expert', split_...  36.5 us
    all_to_all x1, starting transfers between devices, on_device(): lax.all_to_all(out_slots.reshape(experts, slots, width), 'expert', split_...  20.2 us
    dot_general x1, matrix products, on_device(): jnp.einsum('rd,hd->rh', own_grads.reshape(-1, width), w_whole, preferred_...  6.64 us
    unnamed x18, local copies, waits for them, and re-layouts  6.64 us
    dot_general x1, matrix products, on_device(): jnp.dot(hidden[0, 0], w_whole, preferred_element_type=jnp.float32)  6.37 us
    dot_general x1, matrix products, on_device(): jnp.einsum('gsch,sgcd->hd', columns, slot_grads, preferred_element_type=j...  5.17 us
    reshape x1, local copies, waits for them, and re-layouts, on_device(): out_slots.reshape(experts, slots, width)  4.75 us
  transfers between devices with their start and end apart: 4, of which 3 were waited for; matrix products, arithmetic and copies ran while one was open for 22% of the time, Pallas kernels for 0%

commit v1 on v0

v1 whole, which is shorter than its diff:
```python
import jax
import jax.numpy as jnp
from jax import lax
from jax.sharding import PartitionSpec as P

CHUNKS = 2


def slot_ranks(choices, experts):
    flat = choices.reshape(-1)
    onehot = (flat[:, None] == jnp.arange(experts, dtype=jnp.int32)[None, :]).astype(jnp.int32)
    earlier = jnp.cumsum(onehot, axis=0) - onehot
    return jnp.sum(earlier * onehot, axis=1).reshape(choices.shape)


def on_device(hidden, w_down, expert_ids, route_weights, grad_out):
    experts = lax.axis_size("expert")
    groups = lax.axis_size("dp")
    assert groups == 4
    slots = hidden.shape[2] // experts
    width = w_down.shape[2]
    kpart = w_down.shape[1]
    f32, bf16 = jnp.float32, jnp.bfloat16
    d = lax.axis_index("dp")
    parity = d % 2
    half = d // 2
    mate = d + 1 - 2 * parity
    pair_a = [(i, i ^ 1) for i in range(groups)]
    pair_b = [(i, groups - 1 - i) for i in range(groups)]
    hid = hidden[0, 0]
    rows = hid.shape[0]

    def cols(x, k):
        return lax.dynamic_slice_in_dim(x, k * kpart, kpart, axis=1)

    hid_b = lax.ppermute(
        lax.dynamic_slice_in_dim(hid, (1 - half) * 2 * kpart, 2 * kpart, axis=1), "dp", pair_b
    )
    lhs_own = jnp.concatenate([cols(hid, d), cols(hid_b, parity)], axis=0)
    lhs_mate = jnp.concatenate([cols(hid, mate), cols(hid_b, 1 - parity)], axis=0)

    cw = width // CHUNKS
    w_own = w_down[0]
    w_own_c, w_mate_c, out_c = [], [], []
    for c in range(CHUNKS):
        wo = w_own[:, c * cw:(c + 1) * cw]
        wm = lax.ppermute(wo, "dp", pair_a)
        w_own_c.append(wo)
        w_mate_c.append(wm)
        part = jnp.dot(lhs_own, wo, preferred_element_type=f32) + jnp.dot(
            lhs_mate, wm, preferred_element_type=f32
        )
        got = lax.ppermute(part[rows:].astype(bf16), "dp", pair_b)
        out_c.append((part[:rows] + got.astype(f32)).astype(bf16))
    out_slots = jnp.concatenate(out_c, axis=1)

    arrived = lax.all_to_all(
        out_slots.reshape(experts, slots, width), "expert", split_axis=0, concat_axis=0, tiled=True
    )
    arrived = arrived.reshape(experts * slots, width)
    choices = expert_ids[0]
    weights = route_weights[0]
    cotangent = grad_out[0].astype(f32)
    slot_rows = choices * slots + slot_ranks(choices, experts)
    out_pair = arrived[slot_rows].astype(f32)
    mixed = jnp.einsum("tk,tkd->td", weights, out_pair)
    d_route = jnp.einsum("td,tkd->tk", cotangent, out_pair)
    grad_pair = (weights[..., None] * cotangent[:, None, :]).astype(bf16)
    outgoing = jnp.zeros((experts * slots, width), bf16)
    outgoing = outgoing.at[slot_rows.reshape(-1)].set(grad_pair.reshape(-1, width))
    mine = lax.all_to_all(
        outgoing.reshape(experts, slots, width), "expert", split_axis=0, concat_axis=0, tiled=True
    )
    g_own = mine.reshape(experts * slots, width)

    dw_c = []
    dh_own = jnp.zeros((2 * rows, kpart), f32)
    dh_mate = jnp.zeros((2 * rows, kpart), f32)
    for c in range(CHUNKS):
        go = g_own[:, c * cw:(c + 1) * cw]
        gb = lax.ppermute(go, "dp", pair_b)
        g = jnp.concatenate([go, gb], axis=0)
        q_own = jnp.einsum("rh,rd->hd", lhs_own, g, preferred_element_type=f32)
        q_mate = jnp.einsum("rh,rd->hd", lhs_mate, g, preferred_element_type=f32)
        got = lax.ppermute(q_mate.astype(bf16), "dp", pair_a)
        dw_c.append((q_own + got.astype(f32)).astype(bf16))
        dh_own = dh_own + jnp.einsum("rd,hd->rh", g, w_own_c[c], preferred_element_type=f32)
        dh_mate = dh_mate + jnp.einsum("rd,hd->rh", g, w_mate_c[c], preferred_element_type=f32)
    d_weight = jnp.concatenate(dw_c, axis=1)

    dh_own = dh_own.astype(bf16)
    dh_mate = dh_mate.astype(bf16)
    first = parity == 0
    here = jnp.where(first, jnp.concatenate([dh_own, dh_mate], axis=1),
                     jnp.concatenate([dh_mate, dh_own], axis=1))
    there = lax.ppermute(here[rows:], "dp", pair_b)
    d_hidden = jnp.where(half == 0, jnp.concatenate([here[:rows], there], axis=1),
                         jnp.concatenate([there, here[:rows]], axis=1))
    return (
        mixed.astype(bf16)[None],
        d_hidden.reshape(hidden.shape),
        d_weight[None],
        d_route[None],
    )


def solution(mesh):
    placed = (
        P("expert", "dp", None, None),
        P("expert", "dp", None),
        P("dp", "expert", None),
        P("dp", "expert", None),
        P("dp", "expert", None),
    )
    return jax.shard_map(
        on_device,
        mesh=mesh,
        in_specs=placed,
        out_specs=(
            P("dp", "expert", None),
            P("expert", "dp", None, None),
            P("expert", "dp", None),
            P("dp", "expert", None),
        ),
        check_vma=False,
    )
```

time: 198 us -> 217 us (1.096); the launches traced: 198 us -> 213 us
  blocking collectives: 64.9 us -> 0 us
  starting transfers between devices: 24.3 us -> 69.5 us
  waiting for transfers between devices: 42.3 us -> 84.1 us
  between operations: 14.2 us -> 1.11 us
  matrix products: 19.2 us -> 26.1 us
    ppermute x0 -> x10, waiting for transfers between devices: none -> 84.1 us  [the longest x2 32.7 us: on_device(): gb = lax.ppermute(go, 'dp', pair_b)]
    all_to_all x1 -> x0, blocking collectives: 64.9 us -> none  [on_device(): lax.all_to_all(outgoing.reshape(experts, 1, slots, width), 'expert', spli...]
    all_to_all x1, waiting for transfers between devices: 36.5 us -> 0.01 us  [on_device(): lax.all_to_all(out_slots.reshape(experts, slots, width), 'expert', split_...]
    ppermute x0 -> x10, starting transfers between devices: none -> 35.2 us  [the longest x2 11.3 us: on_device(): got = lax.ppermute(part[rows:].astype(bf16), 'dp', pair_b)]
    all_to_all x1, starting transfers between devices: 4.01 us -> 18.8 us  [on_device(): lax.all_to_all(outgoing.reshape(experts, slots, width), 'expert', split_a...]
    dot_general x3 -> x12, matrix products: 18.2 us -> 25.1 us  [the longest x2 6.09 us: on_device(): q_mate = jnp.einsum('rh,rd->hd', lhs_mate, g, preferred_element_type=f32)]
    slice x0 -> x4, local copies, waits for them, and re-layouts: none -> 5.9 us  [the longest x1 2.86 us: on_device(): wo = w_own[:, c * cw:(c + 1) * cw]]
    unnamed x18 -> x13, local copies, waits for them, and re-layouts: 6.64 us -> 1.17 us
  transfers between devices with their start and end apart: 4 -> 12, of which waited for: 3 -> 6; matrix products, arithmetic and copies ran while one was open for 22% -> 24% of each run, Pallas kernels for 0% -> 0%
where the time goes in v1:
time: 217 us; the launch traced here: 213 us
  waiting for transfers between devices  84.1 us (39%)
  starting transfers between devices  69.5 us (32%)
  matrix products  26.1 us (12%)
  local copies, waits for them, and re-layouts  25.8 us (12%)
  other arithmetic  6.52 us (3%)
    ppermute x2, waiting for transfers between devices, on_device(): gb = lax.ppermute(go, 'dp', pair_b)  32.7 us
    ppermute x2, waiting for transfers between devices, on_device(): got = lax.ppermute(part[rows:].astype(bf16), 'dp', pair_b)  29.6 us
    ppermute x2, waiting for transfers between devices, on_device(): got = lax.ppermute(q_mate.astype(bf16), 'dp', pair_a)  21.7 us
    all_to_all x1, starting transfers between devices, on_device(): lax.all_to_all(outgoing.reshape(experts, slots, width), 'expert', split_a...  18.8 us
    all_to_all x1, starting transfers between devices, on_device(): lax.all_to_all(out_slots.reshape(experts, slots, width), 'expert', split_...  15.5 us
    ppermute x2, starting transfers between devices, on_device(): got = lax.ppermute(part[rows:].astype(bf16), 'dp', pair_b)  11.3 us
    ppermute x2, starting transfers between devices, on_device(): gb = lax.ppermute(go, 'dp', pair_b)  6.48 us
    ppermute x2, starting transfers between devices, on_device(): wm = lax.ppermute(wo, 'dp', pair_a)  6.15 us
  transfers between devices with their start and end apart: 12, of which 6 were waited for; matrix products, arithmetic and copies ran while one was open for 24% of the time, Pallas kernels for 0%

profile of v1, /device:TPU:1, one launch (start us, length us, event | category | flops | bytes accessed | tf_op | source)
XLA Modules:
  0.0 213.1 jit_solution(2802599614364514327)
XLA Ops:
  0.7 2.9 %fusion.29 = (bf16[256,1792]{1,0:T(8,128)(2,1)}, bf16[256,1792]{1,0:T(8,128)(2,1)}) fusion(bf16[256,3584]{1,0:T(8,128)(2,1)} %bitcast.54), kind=kLoop, calls=%fused_computation.67 | loop fusion | bytes 3670016 | tf_op jit(solution)/shard_map/slice | solution.py:46
  3.5 3.9 %collective-permute-start.3 = (bf16[256,1792]{1,0:T(8,128)(2,1)}, bf16[256,1792]{1,0:T(8,128)(2,1)}, u32[]{:S(2)}, u32[]{:S(2)}) collective-permute-start(bf16[256,1792]{1,0:T(8,128)(2,1)} %get-tuple-element.15), channel_id=1, source_target_pairs={{0,1},{1,0},{2,3},{3,2},{4,5},{5,4},{6,7},{7,6},{8,9},{9,8},{10,11... | collective-permute-start | bytes 2752520 | tf_op jit(solution)/shard_map/ppermute | solution.py:47
  7.5 3.7 %collective-permute-start = (bf16[256,512]{1,0:T(8,128)(2,1)S(1)}, bf16[256,512]{1,0:T(8,128)(2,1)S(1)}, u32[]{:S(2)}, u32[]{:S(2)}) collective-permute-start(bf16[256,512]{1,0:T(8,128)(2,1)S(1)} %dynamic-slice_bitcast_fusion), channel_id=1, source_target_pairs={{0,3},{1,2},{2,1},{3,0},{4,7},{5,6},{6,5},{7,4},{8,11},{9,10},{10,... | collective-permute-start | bytes 786440 | tf_op jit(solution)/shard_map/ppermute | solution.py:36
  11.3 2.2 %collective-permute-start.1 = (bf16[256,1792]{1,0:T(8,128)(2,1)}, bf16[256,1792]{1,0:T(8,128)(2,1)}, u32[]{:S(2)}, u32[]{:S(2)}) collective-permute-start(bf16[256,1792]{1,0:T(8,128)(2,1)} %get-tuple-element.14), channel_id=1, source_target_pairs={{0,1},{1,0},{2,3},{3,2},{4,5},{5,4},{6,7},{7,6},{8,9},{9,8},{10,11... | collective-permute-start | bytes 2752520 | tf_op jit(solution)/shard_map/ppermute | solution.py:47
  14.5 2.5 %scatter_custom_fusion = bf16[256,3584]{1,0:T(8,128)(2,1)S(1)} fusion(s32[128]{0:T(128)S(1)} %fusion.19, f32[16,3584]{1,0:T(8,128)S(1)} %bitcast_convert_fusion.1, f32[128]{0:T(128)S(1)} %mul.78, bf16[]{:T(256)} %constant.50.clone.1), kind=kCustom, calls=%fused_computation.26 | custom fusion | flops 917504 | bytes 2064898 | tf_op jit(solution)/shard_map/scatter | solution.py:70
  18.7 18.8 %all-to-all-start.1 = ((bf16[128,2,3584]{2,1,0:T(2,128)(2,1)}), bf16[128,2,3584]{2,1,0:T(2,128)(2,1)}, u32[]{:S(2)}, u32[]{:S(2)}) async-start(bf16[128,2,3584]{2,1,0:T(2,128)(2,1)} %reshape.157), calls=%async_computation.1 | async-start | bytes 3670016 | tf_op jit(solution)/shard_map/all_to_all | solution.py:71
  37.7 2.0 fusion.20
  40.5 2.2 %collective-permute-start.4 = (bf16[256,1792]{1,0:T(8,128)(2,1)S(1)}, bf16[256,1792]{1,0:T(8,128)(2,1)S(1)}, u32[]{:S(2)}, u32[]{:S(2)}) collective-permute-start(bf16[256,1792]{1,0:T(8,128)(2,1)S(1)} %slice.72), channel_id=1, source_target_pairs={{0,3},{1,2},{2,1},{3,0},{4,7},{5,6},{6,5},{7,4},{8,11},{9,10},{10,... | collective-permute-start | bytes 2752520 | tf_op jit(solution)/shard_map/ppermute | solution.py:53
  45.4 9.1 %collective-permute-start.2 = (bf16[256,1792]{1,0:T(8,128)(2,1)S(1)}, bf16[256,1792]{1,0:T(8,128)(2,1)S(1)}, u32[]{:S(2)}, u32[]{:S(2)}) collective-permute-start(bf16[256,1792]{1,0:T(8,128)(2,1)S(1)} %slice.73), channel_id=1, source_target_pairs={{0,3},{1,2},{2,1},{3,0},{4,7},{5,6},{6,5},{7,4},{8,11},{9,10},{10,... | collective-permute-start | bytes 2752520 | tf_op jit(solution)/shard_map/ppermute | solution.py:53
  54.5 10.1 %collective-permute-done.4 = bf16[256,1792]{1,0:T(8,128)(2,1)S(1)} collective-permute-done((bf16[256,1792]{1,0:T(8,128)(2,1)S(1)}, bf16[256,1792]{1,0:T(8,128)(2,1)S(1)}, u32[]{:S(2)}, u32[]{:S(2)}) %collective-permute-start.4) | collective-permute-done | bytes 917536 | tf_op jit(solution)/shard_map/ppermute | solution.py:53
  64.8 19.5 %collective-permute-done.2 = bf16[256,1792]{1,0:T(8,128)(2,1)S(1)} collective-permute-done((bf16[256,1792]{1,0:T(8,128)(2,1)S(1)}, bf16[256,1792]{1,0:T(8,128)(2,1)S(1)}, u32[]{:S(2)}, u32[]{:S(2)}) %collective-permute-start.2) | collective-permute-done | bytes 917536 | tf_op jit(solution)/shard_map/ppermute | solution.py:53
  85.8 4.8 %reshape.154 = bf16[128,2,3584]{2,1,0:T(2,128)(2,1)} reshape(bf16[256,3584]{1,0:T(8,128)(2,1)} %pad_maximum_fusion) | data formatting | bytes 3670016 | tf_op jit(solution)/shard_map/reshape | solution.py:58
  90.6 15.5 %all-to-all-start = ((bf16[128,2,3584]{2,1,0:T(2,128)(2,1)}), bf16[128,2,3584]{2,1,0:T(2,128)(2,1)}, u32[]{:S(2)}, u32[]{:S(2)}) async-start(bf16[128,2,3584]{2,1,0:T(2,128)(2,1)} %reshape.154), calls=%async_computation | async-start | bytes 3670016 | tf_op jit(solution)/shard_map/all_to_all | solution.py:57
  106.1 4.9 %reshape.158 = bf16[256,3584]{1,0:T(8,128)(2,1)} reshape(bf16[128,2,3584]{2,1,0:T(2,128)(2,1)} %all-to-all-done.1) | data formatting | bytes 3670016 | tf_op jit(solution)/shard_map/reshape | solution.py:74
  111.0 2.9 %fusion.28 = (bf16[256,1792]{1,0:T(8,128)(2,1)}, bf16[256,1792]{1,0:T(8,128)(2,1)}) fusion(bf16[256,3584]{1,0:T(8,128)(2,1)} %reshape.158), kind=kLoop, calls=%fused_computation.66 | loop fusion | bytes 3670016 | tf_op jit(solution)/shard_map/slice | solution.py:80
  113.9 2.2 %collective-permute-start.6 = (bf16[256,1792]{1,0:T(8,128)(2,1)}, bf16[256,1792]{1,0:T(8,128)(2,1)}, u32[]{:S(2)}, u32[]{:S(2)}) collective-permute-start(bf16[256,1792]{1,0:T(8,128)(2,1)} %get-tuple-element.13), channel_id=1, source_target_pairs={{0,3},{1,2},{2,1},{3,0},{4,7},{5,6},{6,5},{7,4},{8,11},{9,10},{10,... | collective-permute-start | bytes 2752520 | tf_op jit(solution)/shard_map/ppermute | solution.py:81
  116.1 4.2 %collective-permute-start.5 = (bf16[256,1792]{1,0:T(8,128)(2,1)}, bf16[256,1792]{1,0:T(8,128)(2,1)}, u32[]{:S(2)}, u32[]{:S(2)}) collective-permute-start(bf16[256,1792]{1,0:T(8,128)(2,1)} %get-tuple-element.12), channel_id=1, source_target_pairs={{0,3},{1,2},{2,1},{3,0},{4,7},{5,6},{6,5},{7,4},{8,11},{9,10},{10,... | collective-permute-start | bytes 2752520 | tf_op jit(solution)/shard_map/ppermute | solution.py:81
  120.5 17.5 %collective-permute-done.6 = bf16[256,1792]{1,0:T(8,128)(2,1)} collective-permute-done((bf16[256,1792]{1,0:T(8,128)(2,1)}, bf16[256,1792]{1,0:T(8,128)(2,1)}, u32[]{:S(2)}, u32[]{:S(2)}) %collective-permute-start.6) | collective-permute-done | bytes 917536 | tf_op jit(solution)/shard_map/ppermute | solution.py:81
  138.1 2.4 %fusion.22 = f32[512,256]{0,1:T(8,128)S(1)} fusion(bf16[256,1792]{1,0:T(8,128)(2,1)} %collective-permute-done.3, bf16[256,1792]{1,0:T(8,128)(2,1)} %collective-permute-done.6, bf16[256,1792]{1,0:T(8,128)(2,1)} %get-tuple-element.13), kind=kOutput, calls=%fused_computation.60 | convolution fusion | flops 473432064 | bytes 3276800 | tf_op jit(solution)/shard_map/rd,hd->rh/dot_general | solution.py:88
  140.5 2.1 fusion.23
  142.6 15.1 %collective-permute-done.5 = bf16[256,1792]{1,0:T(8,128)(2,1)} collective-permute-done((bf16[256,1792]{1,0:T(8,128)(2,1)}, bf16[256,1792]{1,0:T(8,128)(2,1)}, u32[]{:S(2)}, u32[]{:S(2)}) %collective-permute-start.5) | collective-permute-done | bytes 917536 | tf_op jit(solution)/shard_map/ppermute | solution.py:81
  157.7 2.4 %fusion.6 = bf16[512,256]{0,1:T(8,128)(2,1)S(1)} fusion(f32[512,256]{0,1:T(8,128)S(1)} %fusion.22, bf16[256,1792]{1,0:T(8,128)(2,1)} %collective-permute-done.1, bf16[256,1792]{1,0:T(8,128)(2,1)} %collective-permute-done.5, bf16[256,1792]{1,0:T(8,128)(2,1)} %get-tuple-element.12), kind=kOutput, calls=%fused_computation.25 | convolution fusion | flops 473694208 | bytes 3538944 | tf_op jit(solution)/shard_map/rd,hd->rh/dot_general | solution.py:88
  160.1 2.1 fusion.5
  162.5 2.2 %collective-permute-start.7 = (bf16[256,512]{0,1:T(8,128)(2,1)S(1)}, bf16[256,512]{0,1:T(8,128)(2,1)S(1)}, u32[]{:S(2)}, u32[]{:S(2)}) collective-permute-start(bf16[256,512]{0,1:T(8,128)(2,1)S(1)} %get-tuple-element.17), channel_id=1, source_target_pairs={{0,3},{1,2},{2,1},{3,0},{4,7},{5,6},{6,5},{7,4},{8,11},{9,10},{10,... | collective-permute-start | bytes 786440 | tf_op jit(solution)/shard_map/ppermute | solution.py:96
  164.8 3.0 %convolution_convert_fusion = bf16[256,1792]{1,0:T(8,128)(2,1)} fusion(bf16[256,256]{1,0:T(8,128)(2,1)S(1)} %get-tuple-element.21, bf16[256,256]{1,0:T(8,128)(2,1)S(1)} %get-tuple-element.19, bf16[256,1792]{1,0:T(8,128)(2,1)} %collective-permute-done.6, bf16[256,1792]{1,0:T(8,128)(2,1)} %get-tuple-element.13), kind=kOutput, calls=%fused_computation.6 | convolution fusion | flops 474415104 | bytes 3014656 | tf_op jit(solution)/shard_map/rh,rd->hd/dot_general | solution.py:84
  169.9 3.0 %convolution_convert_fusion.1 = bf16[256,1792]{1,0:T(8,128)(2,1)} fusion(bf16[256,256]{1,0:T(8,128)(2,1)S(1)} %get-tuple-element.21, bf16[256,256]{1,0:T(8,128)(2,1)S(1)} %get-tuple-element.19, bf16[256,1792]{1,0:T(8,128)(2,1)} %collective-permute-done.5, bf16[256,1792]{1,0:T(8,128)(2,1)} %get-tuple-element.12), kind=kOutput, calls=%fused_computation.7 | convolution fusion | flops 474415104 | bytes 3014656 | tf_op jit(solution)/shard_map/rh,rd->hd/dot_general | solution.py:84
  173.0 3.4 %collective-permute-start.8 = (bf16[256,1792]{1,0:T(8,128)(2,1)}, bf16[256,1792]{1,0:T(8,128)(2,1)}, u32[]{:S(2)}, u32[]{:S(2)}) collective-permute-start(bf16[256,1792]{1,0:T(8,128)(2,1)} %convolution_convert_fusion.1), channel_id=1, source_target_pairs={{0,1},{1,0},{2,3},{3,2},{4,5},{5,4},{6,7},{7,6},{8,9},{9,8},{10,11... | collective-permute-start | bytes 2752520 | tf_op jit(solution)/shard_map/ppermute | solution.py:85
  177.7 4.1 %reshape.155 = bf16[256,3584]{1,0:T(8,128)(2,1)S(1)} reshape(bf16[128,2,3584]{2,1,0:T(2,128)(2,1)} %all-to-all-done) | data formatting | bytes 3670016 | tf_op jit(solution)/shard_map/reshape | solution.py:60
  185.2 4.5 %collective-permute-done.9 = bf16[256,1792]{1,0:T(8,128)(2,1)} collective-permute-done((bf16[256,1792]{1,0:T(8,128)(2,1)}, bf16[256,1792]{1,0:T(8,128)(2,1)}, u32[]{:S(2)}, u32[]{:S(2)}) %collective-permute-start.9) | collective-permute-done | bytes 917536 | tf_op jit(solution)/shard_map/ppermute | solution.py:85
  189.7 2.4 %fusion.1 = bf16[256,1792]{1,0:T(8,128)(2,1)S(1)} fusion(bf16[256,1792]{1,0:T(8,128)(2,1)} %collective-permute-done.9, bf16[256,256]{1,0:T(8,128)(2,1)S(1)} %get-tuple-element.20, bf16[256,256]{1,0:T(8,128)(2,1)S(1)} %get-tuple-element.18, bf16[256,1792]{1,0:T(8,128)(2,1)} %collective-permute-done.6, bf16[256,1792]{1,0:T(8,128)(2,1)} %get-tuple-element.13), kind=kOutput, calls=%fused_computation.9 | convolution fusion | flops 475332608 | bytes 3932160 | tf_op jit(solution)/shard_map/rh,rd->hd/dot_general | solution.py:83
  192.1 17.3 %collective-permute-done.8 = bf16[256,1792]{1,0:T(8,128)(2,1)} collective-permute-done((bf16[256,1792]{1,0:T(8,128)(2,1)}, bf16[256,1792]{1,0:T(8,128)(2,1)}, u32[]{:S(2)}, u32[]{:S(2)}) %collective-permute-start.8) | collective-permute-done | bytes 917536 | tf_op jit(solution)/shard_map/ppermute | solution.py:85
  209.3 2.4 %fusion = bf16[256,1792]{1,0:T(8,128)(2,1)S(1)} fusion(bf16[256,1792]{1,0:T(8,128)(2,1)} %collective-permute-done.8, bf16[256,256]{1,0:T(8,128)(2,1)S(1)} %get-tuple-element.20, bf16[256,256]{1,0:T(8,128)(2,1)S(1)} %get-tuple-element.18, bf16[256,1792]{1,0:T(8,128)(2,1)} %collective-permute-done.5, bf16[256,1792]{1,0:T(8,128)(2,1)} %get-tuple-element.12), kind=kOutput, calls=%fused_computation.8 | convolution fusion | flops 475332608 | bytes 3932160 | tf_op jit(solution)/shard_map/rh,rd->hd/dot_general | solution.py:83
  (58 shorter events, 16.4 us)
Async XLA Ops:
  0.6 6.9 %copy-start.1 = (bf16[1,1,256,1024]{3,2,1,0:T(8,128)(2,1)S(1)}, bf16[1,1,256,1024]{3,2,1,0:T(8,128)(2,1)}, u32[]{:S(2)}) copy-start(bf16[1,1,256,1024]{3,2,1,0:T(8,128)(2,1)} %param.5) | copy-start | bytes 1572868
  0.6 12.8 %copy-start.3 = (s32[1,16,8]{1,2,0:T(8,128)S(1)}, s32[1,16,8]{1,2,0:T(8,128)}, u32[]{:S(2)}) copy-start(s32[1,16,8]{1,2,0:T(8,128)} %param.7) | copy-start | bytes 1540
  0.7 13.0 %copy-start.2 = (bf16[1,16,3584]{2,1,0:T(8,128)(2,1)S(1)}, bf16[1,16,3584]{2,1,0:T(8,128)(2,1)}, u32[]{:S(2)}) copy-start(bf16[1,16,3584]{2,1,0:T(8,128)(2,1)} %param.9) | copy-start | bytes 344068
  0.7 13.5 %copy-start.4 = (f32[1,16,8]{1,2,0:T(8,128)S(1)}, f32[1,16,8]{1,2,0:T(8,128)}, u32[]{:S(2)}) copy-start(f32[1,16,8]{1,2,0:T(8,128)} %param.8) | copy-start | bytes 1540
  3.5 34.1 %collective-permute-start.3 = (bf16[256,1792]{1,0:T(8,128)(2,1)}, bf16[256,1792]{1,0:T(8,128)(2,1)}, u32[]{:S(2)}, u32[]{:S(2)}) collective-permute-start(bf16[256,1792]{1,0:T(8,128)(2,1)} %get-tuple-element.15), channel_id=1, source_target_pairs={{0,1},{1,0},{2,3},{3,2},{4,5},{5,4},{6,7},{7,6},{8,9},{9,8},{10,11... | collective-permute-start | bytes 2752520 | tf_op jit(solution)/shard_map/ppermute | solution.py:47
  7.5 30.1 %collective-permute-start = (bf16[256,512]{1,0:T(8,128)(2,1)S(1)}, bf16[256,512]{1,0:T(8,128)(2,1)S(1)}, u32[]{:S(2)}, u32[]{:S(2)}) collective-permute-start(bf16[256,512]{1,0:T(8,128)(2,1)S(1)} %dynamic-slice_bitcast_fusion), channel_id=1, source_target_pairs={{0,3},{1,2},{2,1},{3,0},{4,7},{5,6},{6,5},{7,4},{8,11},{9,10},{10,... | collective-permute-start | bytes 786440 | tf_op jit(solution)/shard_map/ppermute | solution.py:36
  11.3 31.5 %collective-permute-start.1 = (bf16[256,1792]{1,0:T(8,128)(2,1)}, bf16[256,1792]{1,0:T(8,128)(2,1)}, u32[]{:S(2)}, u32[]{:S(2)}) collective-permute-start(bf16[256,1792]{1,0:T(8,128)(2,1)} %get-tuple-element.14), channel_id=1, source_target_pairs={{0,1},{1,0},{2,3},{3,2},{4,5},{5,4},{6,7},{7,6},{8,9},{9,8},{10,11... | collective-permute-start | bytes 2752520 | tf_op jit(solution)/shard_map/ppermute | solution.py:47
  18.7 71.9 %all-to-all-start.1 = ((bf16[128,2,3584]{2,1,0:T(2,128)(2,1)}), bf16[128,2,3584]{2,1,0:T(2,128)(2,1)}, u32[]{:S(2)}, u32[]{:S(2)}) async-start(bf16[128,2,3584]{2,1,0:T(2,128)(2,1)} %reshape.157), calls=%async_computation.1 | async-start | bytes 3670016 | tf_op jit(solution)/shard_map/all_to_all | solution.py:71
  37.7 2.0 copy-start
  40.5 24.2 %collective-permute-start.4 = (bf16[256,1792]{1,0:T(8,128)(2,1)S(1)}, bf16[256,1792]{1,0:T(8,128)(2,1)S(1)}, u32[]{:S(2)}, u32[]{:S(2)}) collective-permute-start(bf16[256,1792]{1,0:T(8,128)(2,1)S(1)} %slice.72), channel_id=1, source_target_pairs={{0,3},{1,2},{2,1},{3,0},{4,7},{5,6},{6,5},{7,4},{8,11},{9,10},{10,... | collective-permute-start | bytes 2752520 | tf_op jit(solution)/shard_map/ppermute | solution.py:53
  45.4 38.9 %collective-permute-start.2 = (bf16[256,1792]{1,0:T(8,128)(2,1)S(1)}, bf16[256,1792]{1,0:T(8,128)(2,1)S(1)}, u32[]{:S(2)}, u32[]{:S(2)}) collective-permute-start(bf16[256,1792]{1,0:T(8,128)(2,1)S(1)} %slice.73), channel_id=1, source_target_pairs={{0,3},{1,2},{2,1},{3,0},{4,7},{5,6},{6,5},{7,4},{8,11},{9,10},{10,... | collective-permute-start | bytes 2752520 | tf_op jit(solution)/shard_map/ppermute | solution.py:53
  90.6 87.0 %all-to-all-start = ((bf16[128,2,3584]{2,1,0:T(2,128)(2,1)}), bf16[128,2,3584]{2,1,0:T(2,128)(2,1)}, u32[]{:S(2)}, u32[]{:S(2)}) async-start(bf16[128,2,3584]{2,1,0:T(2,128)(2,1)} %reshape.154), calls=%async_computation | async-start | bytes 3670016 | tf_op jit(solution)/shard_map/all_to_all | solution.py:57
  113.9 24.2 %collective-permute-start.6 = (bf16[256,1792]{1,0:T(8,128)(2,1)}, bf16[256,1792]{1,0:T(8,128)(2,1)}, u32[]{:S(2)}, u32[]{:S(2)}) collective-permute-start(bf16[256,1792]{1,0:T(8,128)(2,1)} %get-tuple-element.13), channel_id=1, source_target_pairs={{0,3},{1,2},{2,1},{3,0},{4,7},{5,6},{6,5},{7,4},{8,11},{9,10},{10,... | collective-permute-start | bytes 2752520 | tf_op jit(solution)/shard_map/ppermute | solution.py:81
  116.1 41.6 %collective-permute-start.5 = (bf16[256,1792]{1,0:T(8,128)(2,1)}, bf16[256,1792]{1,0:T(8,128)(2,1)}, u32[]{:S(2)}, u32[]{:S(2)}) collective-permute-start(bf16[256,1792]{1,0:T(8,128)(2,1)} %get-tuple-element.12), channel_id=1, source_target_pairs={{0,3},{1,2},{2,1},{3,0},{4,7},{5,6},{6,5},{7,4},{8,11},{9,10},{10,... | collective-permute-start | bytes 2752520 | tf_op jit(solution)/shard_map/ppermute | solution.py:81
  162.5 13.9 %collective-permute-start.7 = (bf16[256,512]{0,1:T(8,128)(2,1)S(1)}, bf16[256,512]{0,1:T(8,128)(2,1)S(1)}, u32[]{:S(2)}, u32[]{:S(2)}) collective-permute-start(bf16[256,512]{0,1:T(8,128)(2,1)S(1)} %get-tuple-element.17), channel_id=1, source_target_pairs={{0,3},{1,2},{2,1},{3,0},{4,7},{5,6},{6,5},{7,4},{8,11},{9,10},{10,... | collective-permute-start | bytes 786440 | tf_op jit(solution)/shard_map/ppermute | solution.py:96
  167.8 21.8 %collective-permute-start.9 = (bf16[256,1792]{1,0:T(8,128)(2,1)}, bf16[256,1792]{1,0:T(8,128)(2,1)}, u32[]{:S(2)}, u32[]{:S(2)}) collective-permute-start(bf16[256,1792]{1,0:T(8,128)(2,1)} %convolution_convert_fusion), channel_id=1, source_target_pairs={{0,1},{1,0},{2,3},{3,2},{4,5},{5,4},{6,7},{7,6},{8,9},{9,8},{10,11... | collective-permute-start | bytes 2752520 | tf_op jit(solution)/shard_map/ppermute | solution.py:85
  173.0 36.4 %collective-permute-start.8 = (bf16[256,1792]{1,0:T(8,128)(2,1)}, bf16[256,1792]{1,0:T(8,128)(2,1)}, u32[]{:S(2)}, u32[]{:S(2)}) collective-permute-start(bf16[256,1792]{1,0:T(8,128)(2,1)} %convolution_convert_fusion.1), channel_id=1, source_target_pairs={{0,1},{1,0},{2,3},{3,2},{4,5},{5,4},{6,7},{7,6},{8,9},{9,8},{10,11... | collective-permute-start | bytes 2752520 | tf_op jit(solution)/shard_map/ppermute | solution.py:85

commit v2 on v1

--- a/solution.py
+++ b/solution.py
@@ -3,7 +3,7 @@
 from jax import lax
 from jax.sharding import PartitionSpec as P
 
-CHUNKS = 2
+CHUNKS = 4
 
 
 def slot_ranks(choices, experts):
@@ -42,15 +42,21 @@
     cw = width // CHUNKS
     w_own = w_down[0]
     w_own_c, w_mate_c, out_c = [], [], []
+    got = None
     for c in range(CHUNKS):
         wo = w_own[:, c * cw:(c + 1) * cw]
+        if c:
+            wo, _ = lax.optimization_barrier((wo, w_mate_c[-1]))
         wm = lax.ppermute(wo, "dp", pair_a)
         w_own_c.append(wo)
         w_mate_c.append(wm)
         part = jnp.dot(lhs_own, wo, preferred_element_type=f32) + jnp.dot(
             lhs_mate, wm, preferred_element_type=f32
         )
-        got = lax.ppermute(part[rows:].astype(bf16), "dp", pair_b)
+        send = part[rows:].astype(bf16)
+        if c:
+            send, _ = lax.optimization_barrier((send, got))
+        got = lax.ppermute(send, "dp", pair_b)
         out_c.append((part[:rows] + got.astype(f32)).astype(bf16))
     out_slots = jnp.concatenate(out_c, axis=1)
 
@@ -76,13 +82,19 @@
     dw_c = []
     dh_own = jnp.zeros((2 * rows, kpart), f32)
     dh_mate = jnp.zeros((2 * rows, kpart), f32)
+    gb = got = None
     for c in range(CHUNKS):
         go = g_own[:, c * cw:(c + 1) * cw]
+        if c:
+            go, _ = lax.optimization_barrier((go, gb))
         gb = lax.ppermute(go, "dp", pair_b)
         g = jnp.concatenate([go, gb], axis=0)
         q_own = jnp.einsum("rh,rd->hd", lhs_own, g, preferred_element_type=f32)
         q_mate = jnp.einsum("rh,rd->hd", lhs_mate, g, preferred_element_type=f32)
-        got = lax.ppermute(q_mate.astype(bf16), "dp", pair_a)
+        send = q_mate.astype(bf16)
+        if c:
+            send, _ = lax.optimization_barrier((send, got))
+        got = lax.ppermute(send, "dp", pair_a)
         dw_c.append((q_own + got.astype(f32)).astype(bf16))
         dh_own = dh_own + jnp.einsum("rd,hd->rh", g, w_own_c[c], preferred_element_type=f32)
         dh_mate = dh_mate + jnp.einsum("rd,hd->rh", g, w_mate_c[c], preferred_element_type=f32)

time: 217 us -> 213 us (0.982)
  the two profiles are of different devices: /device:TPU:1 before, /device:TPU:16 now
where the time goes in v2:
time: 213 us; the launch traced here: 211 us
  starting transfers between devices  86.2 us (40%)
  waiting for transfers between devices  62 us (29%)
  local copies, waits for them, and re-layouts  29.7 us (14%)
  matrix products  22.5 us (11%)
  other arithmetic  9.46 us (4%)
    ppermute x4, waiting for transfers between devices, on_device(): wm = lax.ppermute(wo, 'dp', pair_a)  19.2 us
    all_to_all x1, starting transfers between devices, on_device(): lax.all_to_all(outgoing.reshape(experts, slots, width), 'expert', split_a...  17.4 us
    ppermute x4, waiting for transfers between devices, on_device(): got = lax.ppermute(send, 'dp', pair_b)  16.6 us
    ppermute x4, starting transfers between devices, on_device(): gb = lax.ppermute(go, 'dp', pair_b)  15.9 us
    ppermute x4, waiting for transfers between devices, on_device(): got = lax.ppermute(send, 'dp', pair_a)  15.4 us
    all_to_all x1, starting transfers between devices, on_device(): lax.all_to_all(out_slots.reshape(experts, slots, width), 'expert', split_...  14.3 us
    ppermute x4, starting transfers between devices, on_device(): got = lax.ppermute(send, 'dp', pair_b)  11.5 us
    ppermute x4, starting transfers between devices, on_device(): got = lax.ppermute(send, 'dp', pair_a)  9.33 us
  transfers between devices with their start and end apart: 20, of which 15 were waited for; matrix products, arithmetic and copies ran while one was open for 26% of the time, Pallas kernels for 0%

profile of v2, /device:TPU:16, one launch (start us, length us, event | category | flops | bytes accessed | tf_op | source)
XLA Modules:
  0.0 211.4 jit_solution(1305461336652728067)
XLA Ops:
  2.3 4.7 %collective-permute-start = (bf16[256,512]{1,0:T(8,128)(2,1)}, bf16[256,512]{1,0:T(8,128)(2,1)}, u32[]{:S(2)}, u32[]{:S(2)}) collective-permute-start(bf16[256,512]{1,0:T(8,128)(2,1)} %dynamic-slice_bitcast_fusion), channel_id=1, source_target_pairs={{0,3},{1,2},{2,1},{3,0},{4,7},{5,6},{6,5},{7,4},{8,11},{9,10},{10,... | collective-permute-start | bytes 786440 | tf_op jit(solution)/shard_map/ppermute | solution.py:36
  10.9 2.5 %scatter_custom_fusion = bf16[256,3584]{1,0:T(8,128)(2,1)S(1)} fusion(s32[128]{0:T(128)S(1)} %fusion.27, f32[16,3584]{1,0:T(8,128)S(1)} %bitcast_convert_fusion.1, f32[128]{0:T(128)S(1)} %mul.78, bf16[]{:T(256)} %constant.50.clone.1), kind=kCustom, calls=%fused_computation.30 | custom fusion | flops 917504 | bytes 2064898 | tf_op jit(solution)/shard_map/scatter | solution.py:76
  15.1 17.4 %all-to-all-start.1 = ((bf16[128,2,3584]{2,1,0:T(2,128)(2,1)}), bf16[128,2,3584]{2,1,0:T(2,128)(2,1)S(1)}, u32[]{:S(2)}, u32[]{:S(2)}) async-start(bf16[128,2,3584]{2,1,0:T(2,128)(2,1)} %reshape.157), calls=%async_computation.1 | async-start | bytes 3670016 | tf_op jit(solution)/shard_map/all_to_all | solution.py:77
  32.5 2.4 %fusion.35 = (bf16[256,896]{1,0:T(8,128)(2,1)}, bf16[256,896]{1,0:T(8,128)(2,1)S(1)}, bf16[256,896]{1,0:T(8,128)(2,1)S(1)}, bf16[256,896]{1,0:T(8,128)(2,1)S(1)}) fusion(bf16[256,3584]{1,0:T(8,128)(2,1)} %bitcast.77), kind=kLoop, calls=%fused_computation.88 | loop fusion | bytes 3670016 | tf_op jit(solution)/shard_map/slice | solution.py:47
  39.5 10.1 %collective-permute-done.1 = bf16[256,896]{1,0:T(8,128)(2,1)} collective-permute-done((bf16[256,896]{1,0:T(8,128)(2,1)}, bf16[256,896]{1,0:T(8,128)(2,1)}, u32[]{:S(2)}, u32[]{:S(2)}) %collective-permute-start.1) | collective-permute-done | bytes 458784 | tf_op jit(solution)/shard_map/ppermute | solution.py:50
  54.8 3.0 %collective-permute-start.2 = (bf16[256,896]{1,0:T(8,128)(2,1)S(1)}, bf16[256,896]{1,0:T(8,128)(2,1)S(1)}, u32[]{:S(2)}, u32[]{:S(2)}) collective-permute-start(bf16[256,896]{1,0:T(8,128)(2,1)S(1)} %slice.121), channel_id=1, source_target_pairs={{0,3},{1,2},{2,1},{3,0},{4,7},{5,6},{6,5},{7,4},{8,11},{9,10},{10,... | collective-permute-start | bytes 1376264 | tf_op jit(solution)/shard_map/ppermute | solution.py:59
  57.8 5.4 %collective-permute-done.3 = bf16[256,896]{1,0:T(8,128)(2,1)S(1)} collective-permute-done((bf16[256,896]{1,0:T(8,128)(2,1)S(1)}, bf16[256,896]{1,0:T(8,128)(2,1)S(1)}, u32[]{:S(2)}, u32[]{:S(2)}) %collective-permute-start.3) | collective-permute-done | bytes 458784 | tf_op jit(solution)/shard_map/ppermute | solution.py:50
  63.2 2.3 %collective-permute-start.5 = (bf16[256,896]{1,0:T(8,128)(2,1)S(1)}, bf16[256,896]{1,0:T(8,128)(2,1)S(1)}, u32[]{:S(2)}, u32[]{:S(2)}) collective-permute-start(bf16[256,896]{1,0:T(8,128)(2,1)S(1)} %get-tuple-element.18), channel_id=1, source_target_pairs={{0,1},{1,0},{2,3},{3,2},{4,5},{5,4},{6,7},{7,6},{8,9},{9,8},{10,11... | collective-permute-start | bytes 1376264 | tf_op jit(solution)/shard_map/ppermute | solution.py:50
  66.4 3.0 %collective-permute-done.2 = bf16[256,896]{1,0:T(8,128)(2,1)S(1)} collective-permute-done((bf16[256,896]{1,0:T(8,128)(2,1)S(1)}, bf16[256,896]{1,0:T(8,128)(2,1)S(1)}, u32[]{:S(2)}, u32[]{:S(2)}) %collective-permute-start.2) | collective-permute-done | bytes 458784 | tf_op jit(solution)/shard_map/ppermute | solution.py:59
  69.4 2.9 %collective-permute-start.4 = (bf16[256,896]{1,0:T(8,128)(2,1)S(1)}, bf16[256,896]{1,0:T(8,128)(2,1)S(1)}, u32[]{:S(2)}, u32[]{:S(2)}) collective-permute-start(bf16[256,896]{1,0:T(8,128)(2,1)S(1)} %slice.120), channel_id=1, source_target_pairs={{0,3},{1,2},{2,1},{3,0},{4,7},{5,6},{6,5},{7,4},{8,11},{9,10},{10,... | collective-permute-start | bytes 1376264 | tf_op jit(solution)/shard_map/ppermute | solution.py:59
  73.1 2.8 %collective-permute-done.5 = bf16[256,896]{1,0:T(8,128)(2,1)S(1)} collective-permute-done((bf16[256,896]{1,0:T(8,128)(2,1)S(1)}, bf16[256,896]{1,0:T(8,128)(2,1)S(1)}, u32[]{:S(2)}, u32[]{:S(2)}) %collective-permute-start.5) | collective-permute-done | bytes 458784 | tf_op jit(solution)/shard_map/ppermute | solution.py:50
  75.9 2.3 %collective-permute-start.7 = (bf16[256,896]{1,0:T(8,128)(2,1)S(1)}, bf16[256,896]{1,0:T(8,128)(2,1)S(1)}, u32[]{:S(2)}, u32[]{:S(2)}) collective-permute-start(bf16[256,896]{1,0:T(8,128)(2,1)S(1)} %get-tuple-element.20), channel_id=1, source_target_pairs={{0,1},{1,0},{2,3},{3,2},{4,5},{5,4},{6,7},{7,6},{8,9},{9,8},{10,11... | collective-permute-start | bytes 1376264 | tf_op jit(solution)/shard_map/ppermute | solution.py:50
  79.2 3.9 %collective-permute-done.4 = bf16[256,896]{1,0:T(8,128)(2,1)S(1)} collective-permute-done((bf16[256,896]{1,0:T(8,128)(2,1)S(1)}, bf16[256,896]{1,0:T(8,128)(2,1)S(1)}, u32[]{:S(2)}, u32[]{:S(2)}) %collective-permute-start.4) | collective-permute-done | bytes 458784 | tf_op jit(solution)/shard_map/ppermute | solution.py:59
  83.1 2.8 %collective-permute-start.6 = (bf16[256,896]{1,0:T(8,128)(2,1)S(1)}, bf16[256,896]{1,0:T(8,128)(2,1)S(1)}, u32[]{:S(2)}, u32[]{:S(2)}) collective-permute-start(bf16[256,896]{1,0:T(8,128)(2,1)S(1)} %slice.119), channel_id=1, source_target_pairs={{0,3},{1,2},{2,1},{3,0},{4,7},{5,6},{6,5},{7,4},{8,11},{9,10},{10,... | collective-permute-start | bytes 1376264 | tf_op jit(solution)/shard_map/ppermute | solution.py:59
  89.6 6.4 %collective-permute-done.6 = bf16[256,896]{1,0:T(8,128)(2,1)S(1)} collective-permute-done((bf16[256,896]{1,0:T(8,128)(2,1)S(1)}, bf16[256,896]{1,0:T(8,128)(2,1)S(1)}, u32[]{:S(2)}, u32[]{:S(2)}) %collective-permute-start.6) | collective-permute-done | bytes 458784 | tf_op jit(solution)/shard_map/ppermute | solution.py:59
  96.7 2.8 %collective-permute-start.8 = (bf16[256,896]{1,0:T(8,128)(2,1)}, bf16[256,896]{1,0:T(8,128)(2,1)}, u32[]{:S(2)}, u32[]{:S(2)}) collective-permute-start(bf16[256,896]{1,0:T(8,128)(2,1)} %slice.118), channel_id=1, source_target_pairs={{0,3},{1,2},{2,1},{3,0},{4,7},{5,6},{6,5},{7,4},{8,11},{9,10},{10,... | collective-permute-start | bytes 1376264 | tf_op jit(solution)/shard_map/ppermute | solution.py:59
  101.2 2.7 %fusion.34 = (bf16[256,896]{1,0:T(8,128)(2,1)S(1)}, bf16[256,896]{1,0:T(8,128)(2,1)}, bf16[256,896]{1,0:T(8,128)(2,1)}, bf16[256,896]{1,0:T(8,128)(2,1)}) fusion(bf16[256,3584]{1,0:T(8,128)(2,1)} %reshape.158), kind=kLoop, calls=%fused_computation.87 | loop fusion | bytes 3670016 | tf_op jit(solution)/shard_map/slice | solution.py:87
  103.9 4.5 %collective-permute-start.9 = (bf16[256,896]{1,0:T(8,128)(2,1)S(1)}, bf16[256,896]{1,0:T(8,128)(2,1)S(1)}, u32[]{:S(2)}, u32[]{:S(2)}) collective-permute-start(bf16[256,896]{1,0:T(8,128)(2,1)S(1)} %get-tuple-element.36), channel_id=1, source_target_pairs={{0,3},{1,2},{2,1},{3,0},{4,7},{5,6},{6,5},{7,4},{8,11},{9,10},{10,... | collective-permute-start | bytes 1376264 | tf_op jit(solution)/shard_map/ppermute | solution.py:90
  108.6 3.3 %collective-permute-done.8 = bf16[256,896]{1,0:T(8,128)(2,1)} collective-permute-done((bf16[256,896]{1,0:T(8,128)(2,1)}, bf16[256,896]{1,0:T(8,128)(2,1)}, u32[]{:S(2)}, u32[]{:S(2)}) %collective-permute-start.8) | collective-permute-done | bytes 458784 | tf_op jit(solution)/shard_map/ppermute | solution.py:59
  113.1 5.7 %collective-permute-done.9 = bf16[256,896]{1,0:T(8,128)(2,1)S(1)} collective-permute-done((bf16[256,896]{1,0:T(8,128)(2,1)S(1)}, bf16[256,896]{1,0:T(8,128)(2,1)S(1)}, u32[]{:S(2)}, u32[]{:S(2)}) %collective-permute-start.9) | collective-permute-done | bytes 458784 | tf_op jit(solution)/shard_map/ppermute | solution.py:90
  119.5 2.7 %collective-permute-start.10 = (bf16[256,896]{1,0:T(8,128)(2,1)}, bf16[256,896]{1,0:T(8,128)(2,1)}, u32[]{:S(2)}, u32[]{:S(2)}) collective-permute-start(bf16[256,896]{1,0:T(8,128)(2,1)} %get-tuple-element.22), channel_id=1, source_target_pairs={{0,3},{1,2},{2,1},{3,0},{4,7},{5,6},{6,5},{7,4},{8,11},{9,10},{10,... | collective-permute-start | bytes 1376264 | tf_op jit(solution)/shard_map/ppermute | solution.py:90
  124.1 14.3 %all-to-all-start = ((bf16[128,2,3584]{2,1,0:T(2,128)(2,1)}), bf16[128,2,3584]{2,1,0:T(2,128)(2,1)}, u32[]{:S(2)}, u32[]{:S(2)}) async-start(bf16[128,2,3584]{2,1,0:T(2,128)(2,1)} %reshape.154), calls=%async_computation | async-start | bytes 3670016 | tf_op jit(solution)/shard_map/all_to_all | solution.py:63
  141.9 4.3 %collective-permute-start.11 = (bf16[256,896]{1,0:T(8,128)(2,1)S(1)}, bf16[256,896]{1,0:T(8,128)(2,1)S(1)}, u32[]{:S(2)}, u32[]{:S(2)}) collective-permute-start(bf16[256,896]{1,0:T(8,128)(2,1)S(1)} %copy-done.15), channel_id=1, source_target_pairs={{0,3},{1,2},{2,1},{3,0},{4,7},{5,6},{6,5},{7,4},{8,11},{9,10},{10,... | collective-permute-start | bytes 1376264 | tf_op jit(solution)/shard_map/ppermute | solution.py:90
  148.2 5.1 %collective-permute-done.14 = bf16[256,896]{1,0:T(8,128)(2,1)S(1)} collective-permute-done((bf16[256,896]{1,0:T(8,128)(2,1)S(1)}, bf16[256,896]{1,0:T(8,128)(2,1)S(1)}, u32[]{:S(2)}, u32[]{:S(2)}) %collective-permute-start.14) | collective-permute-done | bytes 458784 | tf_op jit(solution)/shard_map/ppermute | solution.py:97
  157.8 4.3 %collective-permute-start.12 = (bf16[256,896]{1,0:T(8,128)(2,1)S(1)}, bf16[256,896]{1,0:T(8,128)(2,1)S(1)}, u32[]{:S(2)}, u32[]{:S(2)}) collective-permute-start(bf16[256,896]{1,0:T(8,128)(2,1)S(1)} %copy-done.13), channel_id=1, source_target_pairs={{0,3},{1,2},{2,1},{3,0},{4,7},{5,6},{6,5},{7,4},{8,11},{9,10},{10,... | collective-permute-start | bytes 1376264 | tf_op jit(solution)/shard_map/ppermute | solution.py:90
  162.6 4.4 %collective-permute-done.15 = bf16[256,896]{1,0:T(8,128)(2,1)S(1)} collective-permute-done((bf16[256,896]{1,0:T(8,128)(2,1)S(1)}, bf16[256,896]{1,0:T(8,128)(2,1)S(1)}, u32[]{:S(2)}, u32[]{:S(2)}) %collective-permute-start.15) | collective-permute-done | bytes 458784 | tf_op jit(solution)/shard_map/ppermute | solution.py:97
  167.0 2.5 %collective-permute-start.16 = (bf16[256,896]{1,0:T(8,128)(2,1)S(1)}, bf16[256,896]{1,0:T(8,128)(2,1)S(1)}, u32[]{:S(2)}, u32[]{:S(2)}) collective-permute-start(bf16[256,896]{1,0:T(8,128)(2,1)S(1)} %convolution_convert_fusion.1), channel_id=1, source_target_pairs={{0,1},{1,0},{2,3},{3,2},{4,5},{5,4},{6,7},{7,6},{8,9},{9,8},{10,11... | collective-permute-start | bytes 1376264 | tf_op jit(solution)/shard_map/ppermute | solution.py:97
  174.0 5.9 %collective-permute-done.16 = bf16[256,896]{1,0:T(8,128)(2,1)S(1)} collective-permute-done((bf16[256,896]{1,0:T(8,128)(2,1)S(1)}, bf16[256,896]{1,0:T(8,128)(2,1)S(1)}, u32[]{:S(2)}, u32[]{:S(2)}) %collective-permute-start.16) | collective-permute-done | bytes 458784 | tf_op jit(solution)/shard_map/ppermute | solution.py:97
  179.9 2.7 %collective-permute-start.17 = (bf16[256,896]{1,0:T(8,128)(2,1)}, bf16[256,896]{1,0:T(8,128)(2,1)}, u32[]{:S(2)}, u32[]{:S(2)}) collective-permute-start(bf16[256,896]{1,0:T(8,128)(2,1)} %convolution_convert_fusion), channel_id=1, source_target_pairs={{0,1},{1,0},{2,3},{3,2},{4,5},{5,4},{6,7},{7,6},{8,9},{9,8},{10,11... | collective-permute-start | bytes 1376264 | tf_op jit(solution)/shard_map/ppermute | solution.py:97
  186.9 4.3 %collective-permute-start.13 = (bf16[256,512]{0,1:T(8,128)(2,1)S(1)}, bf16[256,512]{0,1:T(8,128)(2,1)S(1)}, u32[]{:S(2)}, u32[]{:S(2)}) collective-permute-start(bf16[256,512]{0,1:T(8,128)(2,1)S(1)} %get-tuple-element.45), channel_id=1, source_target_pairs={{0,3},{1,2},{2,1},{3,0},{4,7},{5,6},{6,5},{7,4},{8,11},{9,10},{10,... | collective-permute-start | bytes 786440 | tf_op jit(solution)/shard_map/ppermute | solution.py:108
  192.5 3.9 %collective-permute-done.13 = bf16[256,512]{0,1:T(8,128)(2,1)S(1)} collective-permute-done((bf16[256,512]{0,1:T(8,128)(2,1)S(1)}, bf16[256,512]{0,1:T(8,128)(2,1)S(1)}, u32[]{:S(2)}, u32[]{:S(2)}) %collective-permute-start.13) | collective-permute-done | bytes 262176 | tf_op jit(solution)/shard_map/ppermute | solution.py:108
  197.6 4.1 %reshape.155 = bf16[256,3584]{1,0:T(8,128)(2,1)S(1)} reshape(bf16[128,2,3584]{2,1,0:T(2,128)(2,1)} %all-to-all-done) | data formatting | bytes 3670016 | tf_op jit(solution)/shard_map/reshape | solution.py:66
  (146 shorter events, 60.7 us)
Async XLA Ops:
  2.3 36.1 %collective-permute-start = (bf16[256,512]{1,0:T(8,128)(2,1)}, bf16[256,512]{1,0:T(8,128)(2,1)}, u32[]{:S(2)}, u32[]{:S(2)}) collective-permute-start(bf16[256,512]{1,0:T(8,128)(2,1)} %dynamic-slice_bitcast_fusion), channel_id=1, source_target_pairs={{0,3},{1,2},{2,1},{3,0},{4,7},{5,6},{6,5},{7,4},{8,11},{9,10},{10,... | collective-permute-start | bytes 786440 | tf_op jit(solution)/shard_map/ppermute | solution.py:36
  15.1 84.4 %all-to-all-start.1 = ((bf16[128,2,3584]{2,1,0:T(2,128)(2,1)}), bf16[128,2,3584]{2,1,0:T(2,128)(2,1)S(1)}, u32[]{:S(2)}, u32[]{:S(2)}) async-start(bf16[128,2,3584]{2,1,0:T(2,128)(2,1)} %reshape.157), calls=%async_computation.1 | async-start | bytes 3670016 | tf_op jit(solution)/shard_map/all_to_all | solution.py:77
  34.9 14.7 %collective-permute-start.1 = (bf16[256,896]{1,0:T(8,128)(2,1)}, bf16[256,896]{1,0:T(8,128)(2,1)}, u32[]{:S(2)}, u32[]{:S(2)}) collective-permute-start(bf16[256,896]{1,0:T(8,128)(2,1)} %get-tuple-element.40), channel_id=1, source_target_pairs={{0,1},{1,0},{2,3},{3,2},{4,5},{5,4},{6,7},{7,6},{8,9},{9,8},{10,11... | collective-permute-start | bytes 1376264 | tf_op jit(solution)/shard_map/ppermute | solution.py:50
  38.4 49.3 %copy-start.6 = (bf16[256,256]{1,0:T(8,128)(2,1)}, bf16[256,256]{1,0:T(8,128)(2,1)S(1)}, u32[]{:S(2)}) copy-start(bf16[256,256]{1,0:T(8,128)(2,1)S(1)} %get-tuple-element.47) | copy-start | bytes 393220
  39.5 48.3 %copy-start.8 = (bf16[256,256]{1,0:T(8,128)(2,1)}, bf16[256,256]{1,0:T(8,128)(2,1)S(1)}, u32[]{:S(2)}) copy-start(bf16[256,256]{1,0:T(8,128)(2,1)S(1)} %get-tuple-element.49) | copy-start | bytes 393220
  49.6 13.6 %collective-permute-start.3 = (bf16[256,896]{1,0:T(8,128)(2,1)S(1)}, bf16[256,896]{1,0:T(8,128)(2,1)S(1)}, u32[]{:S(2)}, u32[]{:S(2)}) collective-permute-start(bf16[256,896]{1,0:T(8,128)(2,1)S(1)} %get-tuple-element.16), channel_id=1, source_target_pairs={{0,1},{1,0},{2,3},{3,2},{4,5},{5,4},{6,7},{7,6},{8,9},{9,8},{10,11... | collective-permute-start | bytes 1376264 | tf_op jit(solution)/shard_map/ppermute | solution.py:50
  54.8 14.6 %collective-permute-start.2 = (bf16[256,896]{1,0:T(8,128)(2,1)S(1)}, bf16[256,896]{1,0:T(8,128)(2,1)S(1)}, u32[]{:S(2)}, u32[]{:S(2)}) collective-permute-start(bf16[256,896]{1,0:T(8,128)(2,1)S(1)} %slice.121), channel_id=1, source_target_pairs={{0,3},{1,2},{2,1},{3,0},{4,7},{5,6},{6,5},{7,4},{8,11},{9,10},{10,... | collective-permute-start | bytes 1376264 | tf_op jit(solution)/shard_map/ppermute | solution.py:59
  63.2 12.7 %collective-permute-start.5 = (bf16[256,896]{1,0:T(8,128)(2,1)S(1)}, bf16[256,896]{1,0:T(8,128)(2,1)S(1)}, u32[]{:S(2)}, u32[]{:S(2)}) collective-permute-start(bf16[256,896]{1,0:T(8,128)(2,1)S(1)} %get-tuple-element.18), channel_id=1, source_target_pairs={{0,1},{1,0},{2,3},{3,2},{4,5},{5,4},{6,7},{7,6},{8,9},{9,8},{10,11... | collective-permute-start | bytes 1376264 | tf_op jit(solution)/shard_map/ppermute | solution.py:50
  69.4 13.7 %collective-permute-start.4 = (bf16[256,896]{1,0:T(8,128)(2,1)S(1)}, bf16[256,896]{1,0:T(8,128)(2,1)S(1)}, u32[]{:S(2)}, u32[]{:S(2)}) collective-permute-start(bf16[256,896]{1,0:T(8,128)(2,1)S(1)} %slice.120), channel_id=1, source_target_pairs={{0,3},{1,2},{2,1},{3,0},{4,7},{5,6},{6,5},{7,4},{8,11},{9,10},{10,... | collective-permute-start | bytes 1376264 | tf_op jit(solution)/shard_map/ppermute | solution.py:59
  75.9 11.9 %collective-permute-start.7 = (bf16[256,896]{1,0:T(8,128)(2,1)S(1)}, bf16[256,896]{1,0:T(8,128)(2,1)S(1)}, u32[]{:S(2)}, u32[]{:S(2)}) collective-permute-start(bf16[256,896]{1,0:T(8,128)(2,1)S(1)} %get-tuple-element.20), channel_id=1, source_target_pairs={{0,1},{1,0},{2,3},{3,2},{4,5},{5,4},{6,7},{7,6},{8,9},{9,8},{10,11... | collective-permute-start | bytes 1376264 | tf_op jit(solution)/shard_map/ppermute | solution.py:50
  79.1 9.1 %copy-start = (f32[512,896]{1,0:T(8,128)}, f32[512,896]{1,0:T(8,128)S(1)}, u32[]{:S(2)}) copy-start(f32[512,896]{1,0:T(8,128)S(1)} %convolution_add_fusion.1) | copy-start | bytes 5505028
  83.1 12.9 %collective-permute-start.6 = (bf16[256,896]{1,0:T(8,128)(2,1)S(1)}, bf16[256,896]{1,0:T(8,128)(2,1)S(1)}, u32[]{:S(2)}, u32[]{:S(2)}) collective-permute-start(bf16[256,896]{1,0:T(8,128)(2,1)S(1)} %slice.119), channel_id=1, source_target_pairs={{0,3},{1,2},{2,1},{3,0},{4,7},{5,6},{6,5},{7,4},{8,11},{9,10},{10,... | collective-permute-start | bytes 1376264 | tf_op jit(solution)/shard_map/ppermute | solution.py:59
  96.7 15.2 %collective-permute-start.8 = (bf16[256,896]{1,0:T(8,128)(2,1)}, bf16[256,896]{1,0:T(8,128)(2,1)}, u32[]{:S(2)}, u32[]{:S(2)}) collective-permute-start(bf16[256,896]{1,0:T(8,128)(2,1)} %slice.118), channel_id=1, source_target_pairs={{0,3},{1,2},{2,1},{3,0},{4,7},{5,6},{6,5},{7,4},{8,11},{9,10},{10,... | collective-permute-start | bytes 1376264 | tf_op jit(solution)/shard_map/ppermute | solution.py:59
  103.9 9.1 %copy-start.4 = (bf16[256,896]{1,0:T(8,128)(2,1)}, bf16[256,896]{1,0:T(8,128)(2,1)S(1)}, u32[]{:S(2)}) copy-start(bf16[256,896]{1,0:T(8,128)(2,1)S(1)} %get-tuple-element.36) | copy-start | bytes 1376260
  103.9 18.3 %copy-start.14 = (bf16[256,896]{1,0:T(8,128)(2,1)S(1)}, bf16[256,896]{1,0:T(8,128)(2,1)}, u32[]{:S(2)}) copy-start(bf16[256,896]{1,0:T(8,128)(2,1)} %fusion.16) | copy-start | bytes 1376260
  103.9 18.3 %copy-start.16 = (bf16[256,896]{1,0:T(8,128)(2,1)S(1)}, bf16[256,896]{1,0:T(8,128)(2,1)}, u32[]{:S(2)}) copy-start(bf16[256,896]{1,0:T(8,128)(2,1)} %fusion.15) | copy-start | bytes 1376260
  103.9 14.8 %collective-permute-start.9 = (bf16[256,896]{1,0:T(8,128)(2,1)S(1)}, bf16[256,896]{1,0:T(8,128)(2,1)S(1)}, u32[]{:S(2)}, u32[]{:S(2)}) collective-permute-start(bf16[256,896]{1,0:T(8,128)(2,1)S(1)} %get-tuple-element.36), channel_id=1, source_target_pairs={{0,3},{1,2},{2,1},{3,0},{4,7},{5,6},{6,5},{7,4},{8,11},{9,10},{10,... | collective-permute-start | bytes 1376264 | tf_op jit(solution)/shard_map/ppermute | solution.py:90
  119.5 22.3 %collective-permute-start.10 = (bf16[256,896]{1,0:T(8,128)(2,1)}, bf16[256,896]{1,0:T(8,128)(2,1)}, u32[]{:S(2)}, u32[]{:S(2)}) collective-permute-start(bf16[256,896]{1,0:T(8,128)(2,1)} %get-tuple-element.22), channel_id=1, source_target_pairs={{0,3},{1,2},{2,1},{3,0},{4,7},{5,6},{6,5},{7,4},{8,11},{9,10},{10,... | collective-permute-start | bytes 1376264 | tf_op jit(solution)/shard_map/ppermute | solution.py:90
  124.1 14.3 %copy-start.5 = (bf16[256,896]{1,0:T(8,128)(2,1)S(1)}, bf16[256,896]{1,0:T(8,128)(2,1)}, u32[]{:S(2)}) copy-start(bf16[256,896]{1,0:T(8,128)(2,1)} %copy-done.4) | copy-start | bytes 1376260
  124.1 14.3 %copy-start.7 = (bf16[256,256]{1,0:T(8,128)(2,1)S(1)}, bf16[256,256]{1,0:T(8,128)(2,1)}, u32[]{:S(2)}) copy-start(bf16[256,256]{1,0:T(8,128)(2,1)} %copy-done.6) | copy-start | bytes 393220
  124.1 14.3 %copy-start.9 = (bf16[256,256]{1,0:T(8,128)(2,1)S(1)}, bf16[256,256]{1,0:T(8,128)(2,1)}, u32[]{:S(2)}) copy-start(bf16[256,256]{1,0:T(8,128)(2,1)} %copy-done.8) | copy-start | bytes 393220
  124.1 14.3 %copy-start.11 = (bf16[256,896]{1,0:T(8,128)(2,1)S(1)}, bf16[256,896]{1,0:T(8,128)(2,1)}, u32[]{:S(2)}) copy-start(bf16[256,896]{1,0:T(8,128)(2,1)} %copy-done.10) | copy-start | bytes 1376260
  124.1 73.5 %all-to-all-start = ((bf16[128,2,3584]{2,1,0:T(2,128)(2,1)}), bf16[128,2,3584]{2,1,0:T(2,128)(2,1)}, u32[]{:S(2)}, u32[]{:S(2)}) async-start(bf16[128,2,3584]{2,1,0:T(2,128)(2,1)} %reshape.154), calls=%async_computation | async-start | bytes 3670016 | tf_op jit(solution)/shard_map/all_to_all | solution.py:63
  138.9 14.4 %collective-permute-start.14 = (bf16[256,896]{1,0:T(8,128)(2,1)S(1)}, bf16[256,896]{1,0:T(8,128)(2,1)S(1)}, u32[]{:S(2)}, u32[]{:S(2)}) collective-permute-start(bf16[256,896]{1,0:T(8,128)(2,1)S(1)} %convolution_convert_fusion.3), channel_id=1, source_target_pairs={{0,1},{1,0},{2,3},{3,2},{4,5},{5,4},{6,7},{7,6},{8,9},{9,8},{10,11... | collective-permute-start | bytes 1376264 | tf_op jit(solution)/shard_map/ppermute | solution.py:97
  141.9 15.7 %collective-permute-start.11 = (bf16[256,896]{1,0:T(8,128)(2,1)S(1)}, bf16[256,896]{1,0:T(8,128)(2,1)S(1)}, u32[]{:S(2)}, u32[]{:S(2)}) collective-permute-start(bf16[256,896]{1,0:T(8,128)(2,1)S(1)} %copy-done.15), channel_id=1, source_target_pairs={{0,3},{1,2},{2,1},{3,0},{4,7},{5,6},{6,5},{7,4},{8,11},{9,10},{10,... | collective-permute-start | bytes 1376264 | tf_op jit(solution)/shard_map/ppermute | solution.py:90
  153.3 13.7 %collective-permute-start.15 = (bf16[256,896]{1,0:T(8,128)(2,1)S(1)}, bf16[256,896]{1,0:T(8,128)(2,1)S(1)}, u32[]{:S(2)}, u32[]{:S(2)}) collective-permute-start(bf16[256,896]{1,0:T(8,128)(2,1)S(1)} %convolution_convert_fusion.2), channel_id=1, source_target_pairs={{0,1},{1,0},{2,3},{3,2},{4,5},{5,4},{6,7},{7,6},{8,9},{9,8},{10,11... | collective-permute-start | bytes 1376264 | tf_op jit(solution)/shard_map/ppermute | solution.py:97
  157.8 14.9 %collective-permute-start.12 = (bf16[256,896]{1,0:T(8,128)(2,1)S(1)}, bf16[256,896]{1,0:T(8,128)(2,1)S(1)}, u32[]{:S(2)}, u32[]{:S(2)}) collective-permute-start(bf16[256,896]{1,0:T(8,128)(2,1)S(1)} %copy-done.13), channel_id=1, source_target_pairs={{0,3},{1,2},{2,1},{3,0},{4,7},{5,6},{6,5},{7,4},{8,11},{9,10},{10,... | collective-permute-start | bytes 1376264 | tf_op jit(solution)/shard_map/ppermute | solution.py:90
  167.0 12.9 %collective-permute-start.16 = (bf16[256,896]{1,0:T(8,128)(2,1)S(1)}, bf16[256,896]{1,0:T(8,128)(2,1)S(1)}, u32[]{:S(2)}, u32[]{:S(2)}) collective-permute-start(bf16[256,896]{1,0:T(8,128)(2,1)S(1)} %convolution_convert_fusion.1), channel_id=1, source_target_pairs={{0,1},{1,0},{2,3},{3,2},{4,5},{5,4},{6,7},{7,6},{8,9},{9,8},{10,11... | collective-permute-start | bytes 1376264 | tf_op jit(solution)/shard_map/ppermute | solution.py:97
  172.7 10.4 %copy-start.20 = (bf16[256,896]{1,0:T(8,128)(2,1)S(1)}, bf16[256,896]{1,0:T(8,128)(2,1)}, u32[]{:S(2)}) copy-start(bf16[256,896]{1,0:T(8,128)(2,1)} %copy-done.19) | copy-start | bytes 1376260
  174.0 9.6 %copy-start.12 = (bf16[256,896]{1,0:T(8,128)(2,1)S(1)}, bf16[256,896]{1,0:T(8,128)(2,1)}, u32[]{:S(2)}) copy-start(bf16[256,896]{1,0:T(8,128)(2,1)} %copy-done.10) | copy-start | bytes 1376260
  179.9 28.6 %collective-permute-start.17 = (bf16[256,896]{1,0:T(8,128)(2,1)}, bf16[256,896]{1,0:T(8,128)(2,1)}, u32[]{:S(2)}, u32[]{:S(2)}) collective-permute-start(bf16[256,896]{1,0:T(8,128)(2,1)} %convolution_convert_fusion), channel_id=1, source_target_pairs={{0,1},{1,0},{2,3},{3,2},{4,5},{5,4},{6,7},{7,6},{8,9},{9,8},{10,11... | collective-permute-start | bytes 1376264 | tf_op jit(solution)/shard_map/ppermute | solution.py:97
  186.9 9.5 %collective-permute-start.13 = (bf16[256,512]{0,1:T(8,128)(2,1)S(1)}, bf16[256,512]{0,1:T(8,128)(2,1)S(1)}, u32[]{:S(2)}, u32[]{:S(2)}) collective-permute-start(bf16[256,512]{0,1:T(8,128)(2,1)S(1)} %get-tuple-element.45), channel_id=1, source_target_pairs={{0,3},{1,2},{2,1},{3,0},{4,7},{5,6},{6,5},{7,4},{8,11},{9,10},{10,... | collective-permute-start | bytes 786440 | tf_op jit(solution)/shard_map/ppermute | solution.py:108
  (18 other events, 81.8 us)

commit v3 on v2

--- a/solution.py
+++ b/solution.py
@@ -40,25 +40,8 @@
     lhs_mate = jnp.concatenate([cols(hid, mate), cols(hid_b, 1 - parity)], axis=0)
 
     cw = width // CHUNKS
-    w_own = w_down[0]
-    w_own_c, w_mate_c, out_c = [], [], []
-    got = None
-    for c in range(CHUNKS):
-        wo = w_own[:, c * cw:(c + 1) * cw]
-        if c:
-            wo, _ = lax.optimization_barrier((wo, w_mate_c[-1]))
-        wm = lax.ppermute(wo, "dp", pair_a)
-        w_own_c.append(wo)
-        w_mate_c.append(wm)
-        part = jnp.dot(lhs_own, wo, preferred_element_type=f32) + jnp.dot(
-            lhs_mate, wm, preferred_element_type=f32
-        )
-        send = part[rows:].astype(bf16)
-        if c:
-            send, _ = lax.optimization_barrier((send, got))
-        got = lax.ppermute(send, "dp", pair_b)
-        out_c.append((part[:rows] + got.astype(f32)).astype(bf16))
-    out_slots = jnp.concatenate(out_c, axis=1)
+    w_whole = lax.all_gather(w_down, "dp", axis=1, tiled=True)[0]
+    out_slots = jnp.dot(hid, w_whole, preferred_element_type=f32).astype(bf16)
 
     arrived = lax.all_to_all(
         out_slots.reshape(experts, slots, width), "expert", split_axis=0, concat_axis=0, tiled=True
@@ -79,9 +62,9 @@
     )
     g_own = mine.reshape(experts * slots, width)
 
+    d_hidden = jnp.einsum("rd,hd->rh", g_own, w_whole, preferred_element_type=f32).astype(bf16)
+    g_own, _ = lax.optimization_barrier((g_own, out_slots))
     dw_c = []
-    dh_own = jnp.zeros((2 * rows, kpart), f32)
-    dh_mate = jnp.zeros((2 * rows, kpart), f32)
     gb = got = None
     for c in range(CHUNKS):
         go = g_own[:, c * cw:(c + 1) * cw]
@@ -96,18 +79,8 @@
             send, _ = lax.optimization_barrier((send, got))
         got = lax.ppermute(send, "dp", pair_a)
         dw_c.append((q_own + got.astype(f32)).astype(bf16))
-        dh_own = dh_own + jnp.einsum("rd,hd->rh", g, w_own_c[c], preferred_element_type=f32)
-        dh_mate = dh_mate + jnp.einsum("rd,hd->rh", g, w_mate_c[c], preferred_element_type=f32)
     d_weight = jnp.concatenate(dw_c, axis=1)
 
-    dh_own = dh_own.astype(bf16)
-    dh_mate = dh_mate.astype(bf16)
-    first = parity == 0
-    here = jnp.where(first, jnp.concatenate([dh_own, dh_mate], axis=1),
-                     jnp.concatenate([dh_mate, dh_own], axis=1))
-    there = lax.ppermute(here[rows:], "dp", pair_b)
-    d_hidden = jnp.where(half == 0, jnp.concatenate([here[:rows], there], axis=1),
-                         jnp.concatenate([there, here[:rows]], axis=1))
     return (
         mixed.astype(bf16)[None],
         d_hidden.reshape(hidden.shape),

time: 213 us -> 214 us (level)
  waiting for transfers between devices: 62 us -> 92.1 us
  starting transfers between devices: 86.2 us -> 60.9 us
  between operations: 1.42 us -> 14.5 us
  local copies, waits for them, and re-layouts: 29.7 us -> 21.8 us
  other arithmetic: 9.46 us -> 4.37 us
  matrix products: 22.5 us -> 19.3 us
    all_to_all x1, waiting for transfers between devices: 0.01 us -> 40.5 us  [on_device(): lax.all_to_all(outgoing.reshape(experts, slots, width), 'expert', split_a...]
    ppermute x9 -> x0, waiting for transfers between devices: 39.7 us -> none  [the longest x4 19.2 us: on_device(): wm = lax.ppermute(wo, 'dp', pair_a)]
    ppermute x9 -> x0, starting transfers between devices: 24.7 us -> none  [the longest x4 11.5 us: on_device(): got = lax.ppermute(send, 'dp', pair_b)]
    all_gather x0 -> x1, waiting for transfers between devices: none -> 19.4 us  [on_device(): w_whole = lax.all_gather(w_down, 'dp', axis=1, tiled=True)[0]]
    ppermute x4, waiting for transfers between devices: 15.4 us -> 25.1 us  [on_device(): got = lax.ppermute(send, 'dp', pair_a)]
    unnamed x66 -> x19, local copies, waits for them, and re-layouts: 5.58 us -> 0.29 us
    slice x5 -> x0, local copies, waits for them, and re-layouts: 3.41 us -> none  [the longest x1 2.37 us: on_device(): wo = w_own[:, c * cw:(c + 1) * cw]]
    reshape x1, local copies, waits for them, and re-layouts: 1.64 us -> 4.76 us  [on_device(): out_slots.reshape(experts, slots, width)]
  transfers between devices with their start and end apart: 20 -> 12, of which waited for: 15 -> 9; matrix products, arithmetic and copies ran while one was open for 26% -> 18% of each run, Pallas kernels for 0% -> 0%
where the time goes in v3:
time: 214 us; the launch traced here: 213 us
  waiting for transfers between devices  92.1 us (43%)
  starting transfers between devices  60.9 us (28%)
  local copies, waits for them, and re-layouts  21.8 us (10%)
  matrix products  19.3 us (9%)
  between operations  14.5 us (7%)
  other arithmetic  4.37 us (2%)
    all_to_all x1, waiting for transfers between devices, on_device(): lax.all_to_all(outgoing.reshape(experts, slots, width), 'expert', split_a...  40.5 us
    ppermute x4, waiting for transfers between devices, on_device(): got = lax.ppermute(send, 'dp', pair_a)  25.1 us
    all_gather x1, waiting for transfers between devices, on_device(): w_whole = lax.all_gather(w_down, 'dp', axis=1, tiled=True)[0]  19.4 us
    all_to_all x1, starting transfers between devices, on_device(): lax.all_to_all(outgoing.reshape(experts, slots, width), 'expert', split_a...  17.9 us
    all_to_all x1, starting transfers between devices, on_device(): lax.all_to_all(out_slots.reshape(experts, slots, width), 'expert', split_...  14.6 us
    ppermute x4, starting transfers between devices, on_device(): gb = lax.ppermute(go, 'dp', pair_b)  14.4 us
    ppermute x4, starting transfers between devices, on_device(): got = lax.ppermute(send, 'dp', pair_a)  9.27 us
    ppermute x4, waiting for transfers between devices, on_device(): gb = lax.ppermute(go, 'dp', pair_b)  6.41 us
  transfers between devices with their start and end apart: 12, of which 9 were waited for; matrix products, arithmetic and copies ran while one was open for 18% of the time, Pallas kernels for 0%

profile of v3, /device:TPU:16, one launch (start us, length us, event | category | flops | bytes accessed | tf_op | source)
XLA Modules:
  0.0 212.9 jit_solution(5786535287300998259)
XLA Ops:
  8.9 2.5 %scatter_custom_fusion = bf16[256,3584]{1,0:T(8,128)(2,1)S(1)} fusion(s32[128]{0:T(128)S(1)} %fusion.31, f32[16,3584]{1,0:T(8,128)S(1)} %bitcast_convert_fusion.1, f32[128]{0:T(128)S(1)} %mul.72, bf16[]{:T(256)} %constant.45.clone.1), kind=kCustom, calls=%fused_computation.24 | custom fusion | flops 917504 | bytes 2064898 | tf_op jit(solution)/shard_map/scatter | solution.py:59
  11.5 1.6 reshape.104
  13.1 17.9 %all-to-all-start.1 = ((bf16[128,2,3584]{2,1,0:T(2,128)(2,1)}), bf16[128,2,3584]{2,1,0:T(2,128)(2,1)}, u32[]{:S(2)}, u32[]{:S(2)}) async-start(bf16[128,2,3584]{2,1,0:T(2,128)(2,1)} %reshape.104), calls=%async_computation.1 | async-start | bytes 3670016 | tf_op jit(solution)/shard_map/all_to_all | solution.py:60
  31.1 4.7 %collective-permute-start = (bf16[256,512]{1,0:T(8,128)(2,1)S(1)}, bf16[256,512]{1,0:T(8,128)(2,1)}, u32[]{:S(2)}, u32[]{:S(2)}) collective-permute-start(bf16[256,512]{1,0:T(8,128)(2,1)S(1)} %dynamic-slice_bitcast_fusion), channel_id=1, source_target_pairs={{0,3},{1,2},{2,1},{3,0},{4,7},{5,6},{6,5},{7,4},{8,11},{9,10},{10,... | collective-permute-start | bytes 786440 | tf_op jit(solution)/shard_map/ppermute | solution.py:36
  35.9 40.5 %all-to-all-done.1 = bf16[128,2,3584]{2,1,0:T(2,128)(2,1)} async-done(((bf16[128,2,3584]{2,1,0:T(2,128)(2,1)}), bf16[128,2,3584]{2,1,0:T(2,128)(2,1)}, u32[]{:S(2)}, u32[]{:S(2)}) %all-to-all-start.1) | async-done | bytes 1835040 | tf_op jit(solution)/shard_map/all_to_all | solution.py:60
  76.4 4.1 %reshape.105 = bf16[256,3584]{1,0:T(8,128)(2,1)S(1)} reshape(bf16[128,2,3584]{2,1,0:T(2,128)(2,1)} %all-to-all-done.1) | data formatting | bytes 3670016 | tf_op jit(solution)/shard_map/reshape | solution.py:63
  80.5 19.4 %all-gather.2.cloned.1.call-done = bf16[1,1024,3584]{2,1,0:T(8,128)(2,1)} async-done(((bf16[1,256,3584]{2,1,0:T(8,128)(2,1)}), bf16[1,1024,3584]{2,1,0:T(8,128)(2,1)}) %all-gather.2.cloned.1.call-update) | async-done | bytes 7340048 | tf_op jit(solution)/shard_map/all_gather | solution.py:43
  99.9 6.4 %fusion.4 = bf16[256,3584]{1,0:T(8,128)(2,1)} fusion(bf16[1,1024,3584]{2,1,0:T(8,128)(2,1)} %all-gather.2.cloned.1.call-done, bf16[1,1,256,1024]{3,2,1,0:T(8,128)(2,1)S(1)} %copy-done), kind=kOutput, calls=%fused_computation.6 | convolution fusion | flops 1879965696 | bytes 9699328 | tf_op jit(solution)/shard_map/dot_general | solution.py:44
  107.2 3.5 %collective-permute-start.1 = (bf16[256,896]{1,0:T(8,128)(2,1)}, bf16[256,896]{1,0:T(8,128)(2,1)}, u32[]{:S(2)}, u32[]{:S(2)}) collective-permute-start(bf16[256,896]{1,0:T(8,128)(2,1)} %get-tuple-element.18), channel_id=1, source_target_pairs={{0,3},{1,2},{2,1},{3,0},{4,7},{5,6},{6,5},{7,4},{8,11},{9,10},{10,... | collective-permute-start | bytes 1376264 | tf_op jit(solution)/shard_map/ppermute | solution.py:73
  111.0 1.7 dynamic-slice_bitcast_fusion.2
  113.7 4.8 %reshape.101 = bf16[128,2,3584]{2,1,0:T(2,128)(2,1)} reshape(bf16[256,3584]{1,0:T(8,128)(2,1)} %fusion.4) | data formatting | bytes 3670016 | tf_op jit(solution)/shard_map/reshape | solution.py:47
  118.5 14.6 %all-to-all-start = ((bf16[128,2,3584]{2,1,0:T(2,128)(2,1)}), bf16[128,2,3584]{2,1,0:T(2,128)(2,1)}, u32[]{:S(2)}, u32[]{:S(2)}) async-start(bf16[128,2,3584]{2,1,0:T(2,128)(2,1)} %reshape.101), calls=%async_computation | async-start | bytes 3670016 | tf_op jit(solution)/shard_map/all_to_all | solution.py:46
  133.1 3.8 %collective-permute-start.3 = (bf16[256,896]{1,0:T(8,128)(2,1)S(1)}, bf16[256,896]{1,0:T(8,128)(2,1)S(1)}, u32[]{:S(2)}, u32[]{:S(2)}) collective-permute-start(bf16[256,896]{1,0:T(8,128)(2,1)S(1)} %get-tuple-element.12), channel_id=1, source_target_pairs={{0,3},{1,2},{2,1},{3,0},{4,7},{5,6},{6,5},{7,4},{8,11},{9,10},{10,... | collective-permute-start | bytes 1376264 | tf_op jit(solution)/shard_map/ppermute | solution.py:73
  137.0 6.0 %fusion.15 = bf16[1,1,256,1024]{3,2,1,0:T(8,128)(2,1)} fusion(bf16[256,3584]{1,0:T(8,128)(2,1)S(1)} %reshape.105, bf16[1,1024,3584]{2,1,0:T(8,128)(2,1)} %all-gather.2.cloned.1.call-done), kind=kOutput, calls=%fused_computation.23 | convolution fusion | flops 1879310336 | bytes 9699328 | tf_op jit(solution)/shard_map/rd,hd->rh/dot_general | solution.py:65
  143.0 1.6 convolution_convert_fusion.3
  144.6 2.1 %collective-permute-start.2 = (bf16[256,896]{1,0:T(8,128)(2,1)S(1)}, bf16[256,896]{1,0:T(8,128)(2,1)S(1)}, u32[]{:S(2)}, u32[]{:S(2)}) collective-permute-start(bf16[256,896]{1,0:T(8,128)(2,1)S(1)} %convolution_convert_fusion.3), channel_id=1, source_target_pairs={{0,1},{1,0},{2,3},{3,2},{4,5},{5,4},{6,7},{7,6},{8,9},{9,8},{10,11... | collective-permute-start | bytes 1376264 | tf_op jit(solution)/shard_map/ppermute | solution.py:80
  146.8 2.1 %collective-permute-done.3 = bf16[256,896]{1,0:T(8,128)(2,1)S(1)} collective-permute-done((bf16[256,896]{1,0:T(8,128)(2,1)S(1)}, bf16[256,896]{1,0:T(8,128)(2,1)S(1)}, u32[]{:S(2)}, u32[]{:S(2)}) %collective-permute-start.3) | collective-permute-done | bytes 458784 | tf_op jit(solution)/shard_map/ppermute | solution.py:73
  148.9 3.5 %collective-permute-start.5 = (bf16[256,896]{1,0:T(8,128)(2,1)S(1)}, bf16[256,896]{1,0:T(8,128)(2,1)S(1)}, u32[]{:S(2)}, u32[]{:S(2)}) collective-permute-start(bf16[256,896]{1,0:T(8,128)(2,1)S(1)} %get-tuple-element.14), channel_id=1, source_target_pairs={{0,3},{1,2},{2,1},{3,0},{4,7},{5,6},{6,5},{7,4},{8,11},{9,10},{10,... | collective-permute-start | bytes 1376264 | tf_op jit(solution)/shard_map/ppermute | solution.py:73
  153.0 5.9 %collective-permute-done.2 = bf16[256,896]{1,0:T(8,128)(2,1)S(1)} collective-permute-done((bf16[256,896]{1,0:T(8,128)(2,1)S(1)}, bf16[256,896]{1,0:T(8,128)(2,1)S(1)}, u32[]{:S(2)}, u32[]{:S(2)}) %collective-permute-start.2) | collective-permute-done | bytes 458784 | tf_op jit(solution)/shard_map/ppermute | solution.py:80
  158.9 2.2 %collective-permute-start.4 = (bf16[256,896]{1,0:T(8,128)(2,1)S(1)}, bf16[256,896]{1,0:T(8,128)(2,1)S(1)}, u32[]{:S(2)}, u32[]{:S(2)}) collective-permute-start(bf16[256,896]{1,0:T(8,128)(2,1)S(1)} %convolution_convert_fusion.2), channel_id=1, source_target_pairs={{0,1},{1,0},{2,3},{3,2},{4,5},{5,4},{6,7},{7,6},{8,9},{9,8},{10,11... | collective-permute-start | bytes 1376264 | tf_op jit(solution)/shard_map/ppermute | solution.py:80
  161.1 1.6 fusion.11
  162.8 1.0 collective-permute-done.5
  163.8 3.5 %collective-permute-start.7 = (bf16[256,896]{1,0:T(8,128)(2,1)S(1)}, bf16[256,896]{1,0:T(8,128)(2,1)S(1)}, u32[]{:S(2)}, u32[]{:S(2)}) collective-permute-start(bf16[256,896]{1,0:T(8,128)(2,1)S(1)} %get-tuple-element.16), channel_id=1, source_target_pairs={{0,3},{1,2},{2,1},{3,0},{4,7},{5,6},{6,5},{7,4},{8,11},{9,10},{10,... | collective-permute-start | bytes 1376264 | tf_op jit(solution)/shard_map/ppermute | solution.py:73
  167.9 4.4 %collective-permute-done.4 = bf16[256,896]{1,0:T(8,128)(2,1)S(1)} collective-permute-done((bf16[256,896]{1,0:T(8,128)(2,1)S(1)}, bf16[256,896]{1,0:T(8,128)(2,1)S(1)}, u32[]{:S(2)}, u32[]{:S(2)}) %collective-permute-start.4) | collective-permute-done | bytes 458784 | tf_op jit(solution)/shard_map/ppermute | solution.py:80
  172.3 2.4 %collective-permute-start.6 = (bf16[256,896]{1,0:T(8,128)(2,1)S(1)}, bf16[256,896]{1,0:T(8,128)(2,1)S(1)}, u32[]{:S(2)}, u32[]{:S(2)}) collective-permute-start(bf16[256,896]{1,0:T(8,128)(2,1)S(1)} %convolution_convert_fusion.1), channel_id=1, source_target_pairs={{0,1},{1,0},{2,3},{3,2},{4,5},{5,4},{6,7},{7,6},{8,9},{9,8},{10,11... | collective-permute-start | bytes 1376264 | tf_op jit(solution)/shard_map/ppermute | solution.py:80
  174.7 3.2 %collective-permute-done.7 = bf16[256,896]{1,0:T(8,128)(2,1)S(1)} collective-permute-done((bf16[256,896]{1,0:T(8,128)(2,1)S(1)}, bf16[256,896]{1,0:T(8,128)(2,1)S(1)}, u32[]{:S(2)}, u32[]{:S(2)}) %collective-permute-start.7) | collective-permute-done | bytes 458784 | tf_op jit(solution)/shard_map/ppermute | solution.py:73
  178.5 6.5 %collective-permute-done.6 = bf16[256,896]{1,0:T(8,128)(2,1)S(1)} collective-permute-done((bf16[256,896]{1,0:T(8,128)(2,1)S(1)}, bf16[256,896]{1,0:T(8,128)(2,1)S(1)}, u32[]{:S(2)}, u32[]{:S(2)}) %collective-permute-start.6) | collective-permute-done | bytes 458784 | tf_op jit(solution)/shard_map/ppermute | solution.py:80
  184.9 2.6 %collective-permute-start.8 = (bf16[256,896]{1,0:T(8,128)(2,1)S(1)}, bf16[256,896]{1,0:T(8,128)(2,1)S(1)}, u32[]{:S(2)}, u32[]{:S(2)}) collective-permute-start(bf16[256,896]{1,0:T(8,128)(2,1)S(1)} %convolution_convert_fusion), channel_id=1, source_target_pairs={{0,1},{1,0},{2,3},{3,2},{4,5},{5,4},{6,7},{7,6},{8,9},{9,8},{10,11... | collective-permute-start | bytes 1376264 | tf_op jit(solution)/shard_map/ppermute | solution.py:80
  188.4 8.3 %collective-permute-done.8 = bf16[256,896]{1,0:T(8,128)(2,1)S(1)} collective-permute-done((bf16[256,896]{1,0:T(8,128)(2,1)S(1)}, bf16[256,896]{1,0:T(8,128)(2,1)S(1)}, u32[]{:S(2)}, u32[]{:S(2)}) %collective-permute-start.8) | collective-permute-done | bytes 458784 | tf_op jit(solution)/shard_map/ppermute | solution.py:80
  197.2 1.4 maximum_bitcast_fusion
  198.6 4.1 %reshape.102 = bf16[256,3584]{1,0:T(8,128)(2,1)S(1)} reshape(bf16[128,2,3584]{2,1,0:T(2,128)(2,1)} %all-to-all-done) | data formatting | bytes 3670016 | tf_op jit(solution)/shard_map/reshape | solution.py:49
  202.6 1.1 gather_fusion
  (57 shorter events, 9.4 us)
Async XLA Ops:
  7.2 0.8 copy-start.5
  7.2 1.0 copy-start.6
  7.2 1.7 copy-start.3
  7.2 92.7 %all-gather.2.cloned.1.call-start = ((), (), s32[]{:S(2)}) async-start(), calls=%async_computation.2 | async-start | bytes 9175040 | tf_op jit(solution)/shard_map/all_gather | solution.py:43
  13.1 17.9 %copy-start = (bf16[1,1,256,1024]{3,2,1,0:T(8,128)(2,1)S(1)}, bf16[1,1,256,1024]{3,2,1,0:T(8,128)(2,1)}, u32[]{:S(2)}) copy-start(bf16[1,1,256,1024]{3,2,1,0:T(8,128)(2,1)} %param.5) | copy-start | bytes 1572868
  13.1 63.3 %all-to-all-start.1 = ((bf16[128,2,3584]{2,1,0:T(2,128)(2,1)}), bf16[128,2,3584]{2,1,0:T(2,128)(2,1)}, u32[]{:S(2)}, u32[]{:S(2)}) async-start(bf16[128,2,3584]{2,1,0:T(2,128)(2,1)} %reshape.104), calls=%async_computation.1 | async-start | bytes 3670016 | tf_op jit(solution)/shard_map/all_to_all | solution.py:60
  31.1 81.6 %collective-permute-start = (bf16[256,512]{1,0:T(8,128)(2,1)S(1)}, bf16[256,512]{1,0:T(8,128)(2,1)}, u32[]{:S(2)}, u32[]{:S(2)}) collective-permute-start(bf16[256,512]{1,0:T(8,128)(2,1)S(1)} %dynamic-slice_bitcast_fusion), channel_id=1, source_target_pairs={{0,3},{1,2},{2,1},{3,0},{4,7},{5,6},{6,5},{7,4},{8,11},{9,10},{10,... | collective-permute-start | bytes 786440 | tf_op jit(solution)/shard_map/ppermute | solution.py:36
  107.2 25.9 %collective-permute-start.1 = (bf16[256,896]{1,0:T(8,128)(2,1)}, bf16[256,896]{1,0:T(8,128)(2,1)}, u32[]{:S(2)}, u32[]{:S(2)}) collective-permute-start(bf16[256,896]{1,0:T(8,128)(2,1)} %get-tuple-element.18), channel_id=1, source_target_pairs={{0,3},{1,2},{2,1},{3,0},{4,7},{5,6},{6,5},{7,4},{8,11},{9,10},{10,... | collective-permute-start | bytes 1376264 | tf_op jit(solution)/shard_map/ppermute | solution.py:73
  118.5 80.1 %all-to-all-start = ((bf16[128,2,3584]{2,1,0:T(2,128)(2,1)}), bf16[128,2,3584]{2,1,0:T(2,128)(2,1)}, u32[]{:S(2)}, u32[]{:S(2)}) async-start(bf16[128,2,3584]{2,1,0:T(2,128)(2,1)} %reshape.101), calls=%async_computation | async-start | bytes 3670016 | tf_op jit(solution)/shard_map/all_to_all | solution.py:46
  133.1 9.8 %copy-start.2 = (bf16[256,256]{1,0:T(8,128)(2,1)S(1)}, bf16[256,256]{1,0:T(8,128)(2,1)}, u32[]{:S(2)}) copy-start(bf16[256,256]{1,0:T(8,128)(2,1)} %get-tuple-element.23) | copy-start | bytes 393220
  133.1 15.8 %collective-permute-start.3 = (bf16[256,896]{1,0:T(8,128)(2,1)S(1)}, bf16[256,896]{1,0:T(8,128)(2,1)S(1)}, u32[]{:S(2)}, u32[]{:S(2)}) collective-permute-start(bf16[256,896]{1,0:T(8,128)(2,1)S(1)} %get-tuple-element.12), channel_id=1, source_target_pairs={{0,3},{1,2},{2,1},{3,0},{4,7},{5,6},{6,5},{7,4},{8,11},{9,10},{10,... | collective-permute-start | bytes 1376264 | tf_op jit(solution)/shard_map/ppermute | solution.py:73
  144.6 16.5 %copy-start.1 = (bf16[256,256]{1,0:T(8,128)(2,1)S(1)}, bf16[256,256]{1,0:T(8,128)(2,1)}, u32[]{:S(2)}) copy-start(bf16[256,256]{1,0:T(8,128)(2,1)} %get-tuple-element.22) | copy-start | bytes 393220
  144.6 14.3 %collective-permute-start.2 = (bf16[256,896]{1,0:T(8,128)(2,1)S(1)}, bf16[256,896]{1,0:T(8,128)(2,1)S(1)}, u32[]{:S(2)}, u32[]{:S(2)}) collective-permute-start(bf16[256,896]{1,0:T(8,128)(2,1)S(1)} %convolution_convert_fusion.3), channel_id=1, source_target_pairs={{0,1},{1,0},{2,3},{3,2},{4,5},{5,4},{6,7},{7,6},{8,9},{9,8},{10,11... | collective-permute-start | bytes 1376264 | tf_op jit(solution)/shard_map/ppermute | solution.py:80
  148.9 14.9 %collective-permute-start.5 = (bf16[256,896]{1,0:T(8,128)(2,1)S(1)}, bf16[256,896]{1,0:T(8,128)(2,1)S(1)}, u32[]{:S(2)}, u32[]{:S(2)}) collective-permute-start(bf16[256,896]{1,0:T(8,128)(2,1)S(1)} %get-tuple-element.14), channel_id=1, source_target_pairs={{0,3},{1,2},{2,1},{3,0},{4,7},{5,6},{6,5},{7,4},{8,11},{9,10},{10,... | collective-permute-start | bytes 1376264 | tf_op jit(solution)/shard_map/ppermute | solution.py:73
  158.9 13.4 %collective-permute-start.4 = (bf16[256,896]{1,0:T(8,128)(2,1)S(1)}, bf16[256,896]{1,0:T(8,128)(2,1)S(1)}, u32[]{:S(2)}, u32[]{:S(2)}) collective-permute-start(bf16[256,896]{1,0:T(8,128)(2,1)S(1)} %convolution_convert_fusion.2), channel_id=1, source_target_pairs={{0,1},{1,0},{2,3},{3,2},{4,5},{5,4},{6,7},{7,6},{8,9},{9,8},{10,11... | collective-permute-start | bytes 1376264 | tf_op jit(solution)/shard_map/ppermute | solution.py:80
  163.8 14.1 %collective-permute-start.7 = (bf16[256,896]{1,0:T(8,128)(2,1)S(1)}, bf16[256,896]{1,0:T(8,128)(2,1)S(1)}, u32[]{:S(2)}, u32[]{:S(2)}) collective-permute-start(bf16[256,896]{1,0:T(8,128)(2,1)S(1)} %get-tuple-element.16), channel_id=1, source_target_pairs={{0,3},{1,2},{2,1},{3,0},{4,7},{5,6},{6,5},{7,4},{8,11},{9,10},{10,... | collective-permute-start | bytes 1376264 | tf_op jit(solution)/shard_map/ppermute | solution.py:73
  172.3 12.6 %collective-permute-start.6 = (bf16[256,896]{1,0:T(8,128)(2,1)S(1)}, bf16[256,896]{1,0:T(8,128)(2,1)S(1)}, u32[]{:S(2)}, u32[]{:S(2)}) collective-permute-start(bf16[256,896]{1,0:T(8,128)(2,1)S(1)} %convolution_convert_fusion.1), channel_id=1, source_target_pairs={{0,1},{1,0},{2,3},{3,2},{4,5},{5,4},{6,7},{7,6},{8,9},{9,8},{10,11... | collective-permute-start | bytes 1376264 | tf_op jit(solution)/shard_map/ppermute | solution.py:80
  184.9 11.8 %collective-permute-start.8 = (bf16[256,896]{1,0:T(8,128)(2,1)S(1)}, bf16[256,896]{1,0:T(8,128)(2,1)S(1)}, u32[]{:S(2)}, u32[]{:S(2)}) collective-permute-start(bf16[256,896]{1,0:T(8,128)(2,1)S(1)} %convolution_convert_fusion), channel_id=1, source_target_pairs={{0,1},{1,0},{2,3},{3,2},{4,5},{5,4},{6,7},{7,6},{8,9},{9,8},{10,11... | collective-permute-start | bytes 1376264 | tf_op jit(solution)/shard_map/ppermute | solution.py:80
  202.6 1.1 copy-start.4
Sparse Core Ops, SparseCore 0:
  10.1 89.7 all-gather.1

commit v4 on v0

--- a/solution.py
+++ b/solution.py
@@ -42,15 +42,19 @@
         tiled=True,
     )
     own_grads = mine[:, 0]
-    slot_grads = lax.all_gather(mine, "dp", axis=1, tiled=True)
     d_hidden = jnp.einsum(
         "rd,hd->rh", own_grads.reshape(-1, width), w_whole, preferred_element_type=jnp.float32
     ).astype(jnp.bfloat16)
     columns = lax.all_to_all(hidden, "dp", split_axis=3, concat_axis=1, tiled=True)[0]
     columns = columns.reshape(groups, experts, slots, columns.shape[-1])
-    d_weight = jnp.einsum(
-        "gsch,sgcd->hd", columns, slot_grads, preferred_element_type=jnp.float32
-    ).astype(jnp.bfloat16)
+    cw = width // 2
+    parts = []
+    for c in range(2):
+        slot_grads = lax.all_gather(mine[..., c * cw:(c + 1) * cw], "dp", axis=1, tiled=True)
+        parts.append(jnp.einsum(
+            "gsch,sgcd->hd", columns, slot_grads, preferred_element_type=jnp.float32
+        ).astype(jnp.bfloat16))
+    d_weight = jnp.concatenate(parts, axis=1)
     return (
         mixed.astype(jnp.bfloat16)[None],
         d_hidden.reshape(hidden.shape),

time: 198 us -> 228 us (1.15)
  waiting for transfers between devices: 42.3 us -> 71.7 us
  starting transfers between devices: 24.3 us -> 20 us
  local copies, waits for them, and re-layouts: 25.9 us -> 29.9 us
    all_gather x1 -> x2, waiting for transfers between devices: 2.96 us -> 70.9 us  [on_device(): lax.all_gather(mine[..., c * cw:(c + 1) * cw], 'dp', axis=1, tiled=True)]
    all_to_all x1, waiting for transfers between devices: 36.5 us -> 0.01 us  [on_device(): lax.all_to_all(out_slots.reshape(experts, slots, width), 'expert', split_...]
    unnamed x18 -> x22, local copies, waits for them, and re-layouts: 6.64 us -> 11.3 us
    all_to_all x1, starting transfers between devices: 20.2 us -> 15.9 us  [on_device(): lax.all_to_all(out_slots.reshape(experts, slots, width), 'expert', split_...]
    all_to_all x1 -> x0, local copies, waits for them, and re-layouts: 3.72 us -> none  [on_device(): lax.all_to_all(outgoing.reshape(experts, 1, slots, width), 'expert', spli...]
    dot_general x1 -> x2, matrix products: 5.17 us -> 6.36 us  [on_device(): jnp.einsum('gsch,sgcd->hd', columns, slot_grads, preferred_element_type=j...]
  transfers between devices with their start and end apart: 4 -> 5, of which waited for: 3 -> 2; matrix products, arithmetic and copies ran while one was open for 22% -> 22% of each run, Pallas kernels for 0% -> 0%
where the time goes in v4:
time: 228 us
  waiting for transfers between devices  71.7 us (31%)
  blocking collectives  64.9 us (28%)
  local copies, waits for them, and re-layouts  29.9 us (13%)
  matrix products  20.3 us (9%)
  starting transfers between devices  20 us (9%)
  between operations  14 us (6%)
  other arithmetic  6.95 us (3%)
    all_gather x2, waiting for transfers between devices, on_device(): lax.all_gather(mine[..., c * cw:(c + 1) * cw], 'dp', axis=1, tiled=True)  70.9 us
    all_to_all x1, blocking collectives, on_device(): lax.all_to_all(outgoing.reshape(experts, 1, slots, width), 'expert', spli...  64.9 us
    all_to_all x1, starting transfers between devices, on_device(): lax.all_to_all(out_slots.reshape(experts, slots, width), 'expert', split_...  15.9 us
    unnamed x22, local copies, waits for them, and re-layouts  11.3 us
    dot_general x1, matrix products, on_device(): jnp.einsum('rd,hd->rh', own_grads.reshape(-1, width), w_whole, preferred_...  6.53 us
    dot_general x1, matrix products, on_device(): jnp.dot(hidden[0, 0], w_whole, preferred_element_type=jnp.float32)  6.37 us
    dot_general x2, matrix products, on_device(): jnp.einsum('gsch,sgcd->hd', columns, slot_grads, preferred_element_type=j...  6.36 us
    reshape x1, local copies, waits for them, and re-layouts, on_device(): out_slots.reshape(experts, slots, width)  4.77 us
  transfers between devices with their start and end apart: 5, of which 2 were waited for; matrix products, arithmetic and copies ran while one was open for 22% of the time, Pallas kernels for 0%

profile of v4, /device:TPU:1, one launch (start us, length us, event | category | flops | bytes accessed | tf_op | source)
XLA Modules:
  0.0 227.6 jit_solution(7683013739206800182)
XLA Ops:
  7.2 0.7 all-gather.4.cloned.1.call-update
  8.6 0.2 reduce_window_sum.11
  8.8 0.2 select_reduce_fusion
  9.0 2.5 %scatter_custom_fusion = bf16[256,3584]{1,0:T(8,128)(2,1)S(1)} fusion(s32[128]{0:T(128)S(1)} %fusion.33, f32[16,3584]{1,0:T(8,128)S(1)} %bitcast_convert_fusion.1, f32[128]{0:T(128)S(1)} %mul.53, bf16[]{:T(256)} %constant.7.clone.1), kind=kCustom, calls=%fused_computation.18 | custom fusion | flops 917504 | bytes 2064898 | tf_op jit(solution)/shard_map/scatter | solution.py:36
  11.5 1.6 reshape.99
  13.2 64.9 %all_to_all.25 = bf16[128,1,2,3584]{3,2,1,0:T(2,128)(2,1)S(1)} all-to-all(bf16[128,1,2,3584]{3,2,1,0:T(2,128)(2,1)} %bitcast.87), channel_id=1, replica_groups=mesh['expert'=128,'dp'=4] {'expert'}, dimensions={0} | all-to-all | bytes 3670016 | tf_op jit(solution)/shard_map/all_to_all | solution.py:37
  78.1 2.2 fusion.34
  80.2 3.6 %copy.71 = bf16[128,1,2,1792]{0,3,1,2:T(8,128)(2,1)} copy(bf16[128,1,2,1792]{3,2,1,0:T(2,128)(2,1)} %get-tuple-element.24) | data formatting | bytes 1835008
  83.9 2.1 copy.72
  86.0 0.9 copy.58
  86.9 0.5 broadcast.58
  87.4 3.8 %reduce = bf16[1024,256]{1,0:T(8,128)(2,1)S(1)} reduce(bf16[1024,1,1,256]{3,2,1,0:T(2,128)(2,1)S(1)} %bitcast.89, bf16[]{:T(256)} %broadcast.58), dimensions={1,2}, to_apply=%bitcast.78.reduce_sub_computation | reduce | bytes 1048578
  91.3 0.9 reshape.126
  92.2 4.0 %all-to-all-start.2 = ((bf16[4,2,32768]{2,1,0:T(2,128)(2,1)}), bf16[4,2,32768]{2,1,0:T(2,128)(2,1)S(1)}, u32[]{:S(2)}, u32[]{:S(2)}) async-start(bf16[4,2,32768]{2,1,0:T(2,128)(2,1)} %reshape.126), calls=%async_computation.2 | async-start | bytes 1048576 | tf_op jit(solution)/shard_map/all_to_all | solution.py:48
  96.2 6.4 %fusion.4 = bf16[256,3584]{1,0:T(8,128)(2,1)} fusion(bf16[1,1024,3584]{2,1,0:T(8,128)(2,1)} %all-gather.4.cloned.1.call-done, bf16[1,1,256,1024]{3,2,1,0:T(8,128)(2,1)S(1)} %copy-done.1), kind=kOutput, calls=%fused_computation.6 | convolution fusion | flops 1879965696 | bytes 9699328 | tf_op jit(solution)/shard_map/dot_general | solution.py:20
  102.6 4.8 %reshape.96 = bf16[128,2,3584]{2,1,0:T(2,128)(2,1)} reshape(bf16[256,3584]{1,0:T(8,128)(2,1)} %fusion.4) | data formatting | bytes 3670016 | tf_op jit(solution)/shard_map/reshape | solution.py:24
  107.3 15.9 %all-to-all-start = ((bf16[128,2,3584]{2,1,0:T(2,128)(2,1)}), bf16[128,2,3584]{2,1,0:T(2,128)(2,1)}, u32[]{:S(2)}, u32[]{:S(2)}) async-start(bf16[128,2,3584]{2,1,0:T(2,128)(2,1)} %reshape.96), calls=%async_computation | async-start | bytes 3670016 | tf_op jit(solution)/shard_map/all_to_all | solution.py:23
  123.6 0.5 reshape.127
  124.3 1.1 copy.59
  125.3 1.7 reshape_squeeze.6
  127.0 22.5 %all-gather.6.cloned.1.call-done = bf16[128,4,2,1792]{0,3,1,2:T(8,128)(2,1)} async-done(((bf16[128,1,2,1792]{0,3,1,2:T(8,128)(2,1)}), bf16[128,4,2,1792]{0,3,1,2:T(8,128)(2,1)}) %all-gather.6.cloned.1.call-update) | async-done | bytes 3670032 | tf_op jit(solution)/shard_map/all_gather | solution.py:53
  149.5 3.2 %fusion.10 = bf16[256,1792]{0,1:T(8,128)(2,1)S(1)} fusion(bf16[128,4,2,1792]{0,3,1,2:T(8,128)(2,1)} %all-gather.6.cloned.1.call-done, bf16[4,128,2,256]{3,0,2,1:T(4,128)(2,1)S(1)} %bitcast.91), kind=kOutput, calls=%fused_computation.12 | convolution fusion | flops 939982848 | bytes 5111808 | tf_op jit(solution)/shard_map/gsch,sgcd->hd/dot_general | solution.py:54
  152.7 48.4 %all-gather.8.cloned.1.call-done = bf16[128,4,2,1792]{0,3,1,2:T(8,128)(2,1)} async-done(((bf16[128,1,2,1792]{0,3,1,2:T(8,128)(2,1)}), bf16[128,4,2,1792]{0,3,1,2:T(8,128)(2,1)}) %all-gather.8.cloned.1.call-update) | async-done | bytes 3670032 | tf_op jit(solution)/shard_map/all_gather | solution.py:53
  201.1 3.2 %fusion.9 = bf16[256,1792]{0,1:T(8,128)(2,1)S(1)} fusion(bf16[128,4,2,1792]{0,3,1,2:T(8,128)(2,1)} %all-gather.8.cloned.1.call-done, bf16[4,128,2,256]{3,0,2,1:T(4,128)(2,1)S(1)} %bitcast.92), kind=kOutput, calls=%fused_computation.11 | convolution fusion | flops 939982848 | bytes 5111808 | tf_op jit(solution)/shard_map/gsch,sgcd->hd/dot_general | solution.py:54
  204.4 2.6 %copy.63 = bf16[1,256,3584]{2,1,0:T(8,128)(2,1)} copy(bf16[1,256,3584]{1,2,0:T(8,128)(2,1)S(1)} %maximum_bitcast_fusion) | data formatting | bytes 3670016
  207.0 6.5 %fusion.15 = bf16[1,1,256,1024]{3,2,1,0:T(8,128)(2,1)} fusion(bf16[256,3584]{1,0:T(8,128)(2,1)} %reshape_squeeze.6, bf16[1,1024,3584]{2,1,0:T(8,128)(2,1)} %all-gather.4.cloned.1.call-done), kind=kOutput, calls=%fused_computation.17 | convolution fusion | flops 1879310336 | bytes 9699328 | tf_op jit(solution)/shard_map/rd,hd->rh/dot_general | solution.py:45
  213.5 4.1 %reshape.97 = bf16[256,3584]{1,0:T(8,128)(2,1)S(1)} reshape(bf16[128,2,3584]{2,1,0:T(2,128)(2,1)} %all-to-all-done) | data formatting | bytes 3670016 | tf_op jit(solution)/shard_map/reshape | solution.py:26
  217.6 1.1 gather_fusion
  218.7 0.6 fusion.22
  219.3 0.4 fusion.20
  219.7 0.7 copy.82
  220.4 0.7 copy.69
  (39 shorter events, 1.4 us)
Async XLA Ops:
  7.2 0.8 copy-start.4
  7.2 1.1 copy-start.5
  7.2 1.8 copy-start.3
  7.2 89.0 %all-gather.4.cloned.1.call-start = ((), (), s32[]{:S(2)}) async-start(), calls=%async_computation.3 | async-start | bytes 9175040 | tf_op jit(solution)/shard_map/all_gather | solution.py:19
  7.9 141.6 %all-gather.6.cloned.1.call-start = ((), (), s32[]{:S(2)}) async-start(), calls=%async_computation.4 | async-start | bytes 4587520 | tf_op jit(solution)/shard_map/all_gather | solution.py:53
  83.8 2.2 copy-start
  83.8 117.3 %all-gather.8.cloned.1.call-start = ((), (), s32[]{:S(2)}) async-start(), calls=%async_computation.5 | async-start | bytes 4587520 | tf_op jit(solution)/shard_map/all_gather | solution.py:53
  91.3 4.9 %copy-start.1 = (bf16[1,1,256,1024]{3,2,1,0:T(8,128)(2,1)S(1)}, bf16[1,1,256,1024]{3,2,1,0:T(8,128)(2,1)}, u32[]{:S(2)}) copy-start(bf16[1,1,256,1024]{3,2,1,0:T(8,128)(2,1)} %param.5) | copy-start | bytes 1572868
  92.2 15.2 %all-to-all-start.2 = ((bf16[4,2,32768]{2,1,0:T(2,128)(2,1)}), bf16[4,2,32768]{2,1,0:T(2,128)(2,1)S(1)}, u32[]{:S(2)}, u32[]{:S(2)}) async-start(bf16[4,2,32768]{2,1,0:T(2,128)(2,1)} %reshape.126), calls=%async_computation.2 | async-start | bytes 1048576 | tf_op jit(solution)/shard_map/all_to_all | solution.py:48
  107.3 106.2 %all-to-all-start = ((bf16[128,2,3584]{2,1,0:T(2,128)(2,1)}), bf16[128,2,3584]{2,1,0:T(2,128)(2,1)}, u32[]{:S(2)}, u32[]{:S(2)}) async-start(bf16[128,2,3584]{2,1,0:T(2,128)(2,1)} %reshape.96), calls=%async_computation | async-start | bytes 3670016 | tf_op jit(solution)/shard_map/all_to_all | solution.py:23
  125.3 24.2 %copy-start.2 = (bf16[1,4,1,256,256]{4,1,3,2,0:T(4,128)(2,1)S(1)}, bf16[1,4,1,256,256]{4,1,3,2,0:T(4,128)(2,1)}, u32[]{:S(2)}) copy-start(bf16[1,4,1,256,256]{4,1,3,2,0:T(4,128)(2,1)} %copy.59) | copy-start | bytes 1572868
Sparse Core Ops, SparseCore 0:
  10.1 84.9 all-gather.3
  97.2 52.2 all-gather.5
  151.6 49.4 all-gather.7

commit v5 on v3

--- a/solution.py
+++ b/solution.py
@@ -63,19 +63,28 @@
     g_own = mine.reshape(experts * slots, width)
 
     d_hidden = jnp.einsum("rd,hd->rh", g_own, w_whole, preferred_element_type=f32).astype(bf16)
+    cw = width // CHUNKS
+    split = width // 2
+    columns = lax.all_to_all(hidden, "dp", split_axis=3, concat_axis=1, tiled=True)[0]
+    columns = columns.reshape(groups, experts, slots, columns.shape[-1])
+    slot_grads = lax.all_gather(
+        mine.reshape(experts, 1, slots, width)[..., :split], "dp", axis=1, tiled=True
+    )
+    dw_c = [jnp.einsum(
+        "gsch,sgcd->hd", columns, slot_grads, preferred_element_type=f32
+    ).astype(bf16)]
     g_own, _ = lax.optimization_barrier((g_own, out_slots))
-    dw_c = []
     gb = got = None
-    for c in range(CHUNKS):
+    for c in range(split // cw, CHUNKS):
         go = g_own[:, c * cw:(c + 1) * cw]
-        if c:
+        if gb is not None:
             go, _ = lax.optimization_barrier((go, gb))
         gb = lax.ppermute(go, "dp", pair_b)
         g = jnp.concatenate([go, gb], axis=0)
         q_own = jnp.einsum("rh,rd->hd", lhs_own, g, preferred_element_type=f32)
         q_mate = jnp.einsum("rh,rd->hd", lhs_mate, g, preferred_element_type=f32)
         send = q_mate.astype(bf16)
-        if c:
+        if got is not None:
             send, _ = lax.optimization_barrier((send, got))
         got = lax.ppermute(send, "dp", pair_a)
         dw_c.append((q_own + got.astype(f32)).astype(bf16))

time: 214 us -> 214 us (level)
  the two profiles are of different devices: /device:TPU:16 before, /device:TPU:1 now
where the time goes in v5:
time: 214 us; the launch traced here: 212 us
  blocking collectives  64.9 us (30%)
  starting transfers between devices  36 us (17%)
  waiting for transfers between devices  34.4 us (16%)
  local copies, waits for them, and re-layouts  33.4 us (16%)
  matrix products  20.9 us (10%)
  between operations  14.4 us (7%)
  other arithmetic  7.74 us (4%)
    all_to_all x1, blocking collectives, on_device(): lax.all_to_all(outgoing.reshape(experts, slots, width), 'expert', split_a...  64.9 us
    ppermute x2, waiting for transfers between devices, on_device(): gb = lax.ppermute(go, 'dp', pair_b)  18.9 us
    all_to_all x1, starting transfers between devices, on_device(): lax.all_to_all(out_slots.reshape(experts, slots, width), 'expert', split_...  16.3 us
    ppermute x2, waiting for transfers between devices, on_device(): got = lax.ppermute(send, 'dp', pair_a)  8.57 us
    unnamed x25, local copies, waits for them, and re-layouts  6.77 us
    ppermute x2, starting transfers between devices, on_device(): gb = lax.ppermute(go, 'dp', pair_b)  6.48 us
    dot_general x1, matrix products, on_device(): out_slots = jnp.dot(hid, w_whole, preferred_element_type=f32).astype(bf16)  6.37 us
    dot_general x1, matrix products, on_device(): jnp.einsum('rd,hd->rh', g_own, w_whole, preferred_element_type=f32)  5.98 us
  transfers between devices with their start and end apart: 9, of which 6 were waited for; matrix products, arithmetic and copies ran while one was open for 26% of the time, Pallas kernels for 0%

profile of v5, /device:TPU:1, one launch (start us, length us, event | category | flops | bytes accessed | tf_op | source)
XLA Modules:
  0.0 211.8 jit_solution(3337184370189462294)
XLA Ops:
  9.0 2.5 %scatter_custom_fusion = bf16[256,3584]{1,0:T(8,128)(2,1)S(1)} fusion(s32[128]{0:T(128)S(1)} %fusion.32, f32[16,3584]{1,0:T(8,128)S(1)} %bitcast_convert_fusion.1, f32[128]{0:T(128)S(1)} %mul.72, bf16[]{:T(256)} %constant.45.clone.1), kind=kCustom, calls=%fused_computation.21 | custom fusion | flops 917504 | bytes 2064898 | tf_op jit(solution)/shard_map/scatter | solution.py:59
  11.5 1.6 reshape.108
  13.2 64.9 %all_to_all.25 = bf16[128,2,3584]{2,1,0:T(2,128)(2,1)S(1)} all-to-all(bf16[128,2,3584]{2,1,0:T(2,128)(2,1)} %reshape.108), channel_id=1, replica_groups=mesh['expert'=128,'dp'=4] {'expert'}, dimensions={0} | all-to-all | bytes 3670016 | tf_op jit(solution)/shard_map/all_to_all | solution.py:60
  78.1 3.7 %copy.51 = bf16[128,2,3584]{0,2,1:T(8,128)(2,1)} copy(bf16[128,2,3584]{2,1,0:T(2,128)(2,1)S(1)} %all_to_all.25) | data formatting | bytes 3670016 | tf_op jit(solution)/shard_map/all_to_all | solution.py:60
  81.7 2.2 %slice.14 = bf16[128,1,2,1792]{0,3,1,2:T(8,128)(2,1)} slice(bf16[128,1,2,3584]{0,3,1,2:T(8,128)(2,1)} %bitcast.85), slice={[0:128], [0:1], [0:2], [0:1792]} | slice | bytes 1835008 | tf_op jit(solution)/shard_map/slice | solution.py:71
  84.0 0.9 copy.52
  85.4 4.6 %reduce = bf16[1024,256]{1,0:T(8,128)(2,1)} reduce(bf16[1024,1,1,256]{3,2,1,0:T(2,128)(2,1)S(1)} %bitcast.84, bf16[]{:T(256)} %broadcast.60), dimensions={1,2}, to_apply=%bitcast.74.reduce_sub_computation | reduce | bytes 1048578
  90.0 2.0 reshape.136
  92.0 4.0 %all-to-all-start.2 = ((bf16[4,2,32768]{2,1,0:T(2,128)(2,1)}), bf16[4,2,32768]{2,1,0:T(2,128)(2,1)S(1)}, u32[]{:S(2)}, u32[]{:S(2)}) async-start(bf16[4,2,32768]{2,1,0:T(2,128)(2,1)} %reshape.136), calls=%async_computation.2 | async-start | bytes 1048576 | tf_op jit(solution)/shard_map/all_to_all | solution.py:68
  96.0 6.4 %fusion.4 = bf16[256,3584]{1,0:T(8,128)(2,1)} fusion(bf16[1,1024,3584]{2,1,0:T(8,128)(2,1)} %all-gather.3.cloned.1.call-done, bf16[1,1,256,1024]{3,2,1,0:T(8,128)(2,1)S(1)} %copy-done.1), kind=kOutput, calls=%fused_computation.6 | convolution fusion | flops 1879965696 | bytes 9699328 | tf_op jit(solution)/shard_map/dot_general | solution.py:44
  102.4 4.8 %reshape.105 = bf16[128,2,3584]{2,1,0:T(2,128)(2,1)} reshape(bf16[256,3584]{1,0:T(8,128)(2,1)} %fusion.4) | data formatting | bytes 3670016 | tf_op jit(solution)/shard_map/reshape | solution.py:47
  107.2 16.3 %all-to-all-start = ((bf16[128,2,3584]{2,1,0:T(2,128)(2,1)}), bf16[128,2,3584]{2,1,0:T(2,128)(2,1)}, u32[]{:S(2)}, u32[]{:S(2)}) async-start(bf16[128,2,3584]{2,1,0:T(2,128)(2,1)} %reshape.105), calls=%async_computation | async-start | bytes 3670016 | tf_op jit(solution)/shard_map/all_to_all | solution.py:46
  124.2 3.6 %collective-permute-start = (bf16[256,512]{1,0:T(8,128)(2,1)}, bf16[256,512]{1,0:T(8,128)(2,1)}, u32[]{:S(2)}, u32[]{:S(2)}) collective-permute-start(bf16[256,512]{1,0:T(8,128)(2,1)} %dynamic-slice_bitcast_fusion), channel_id=1, source_target_pairs={{0,3},{1,2},{2,1},{3,0},{4,7},{5,6},{6,5},{7,4},{8,11},{9,10},{10,... | collective-permute-start | bytes 786440 | tf_op jit(solution)/shard_map/ppermute | solution.py:36
  128.0 1.6 reshape.109
  129.7 2.0 fusion.37
  131.7 2.9 %collective-permute-start.1 = (bf16[256,896]{1,0:T(8,128)(2,1)}, bf16[256,896]{1,0:T(8,128)(2,1)}, u32[]{:S(2)}, u32[]{:S(2)}) collective-permute-start(bf16[256,896]{1,0:T(8,128)(2,1)} %get-tuple-element.26), channel_id=1, source_target_pairs={{0,3},{1,2},{2,1},{3,0},{4,7},{5,6},{6,5},{7,4},{8,11},{9,10},{10,... | collective-permute-start | bytes 1376264 | tf_op jit(solution)/shard_map/ppermute | solution.py:82
  135.6 5.7 %collective-permute-done = bf16[256,512]{1,0:T(8,128)(2,1)} collective-permute-done((bf16[256,512]{1,0:T(8,128)(2,1)}, bf16[256,512]{1,0:T(8,128)(2,1)}, u32[]{:S(2)}, u32[]{:S(2)}) %collective-permute-start) | collective-permute-done | bytes 262176 | tf_op jit(solution)/shard_map/ppermute | solution.py:36
  141.3 1.6 constant_dynamic-slice_fusion
  143.8 17.1 %collective-permute-done.1 = bf16[256,896]{1,0:T(8,128)(2,1)} collective-permute-done((bf16[256,896]{1,0:T(8,128)(2,1)}, bf16[256,896]{1,0:T(8,128)(2,1)}, u32[]{:S(2)}, u32[]{:S(2)}) %collective-permute-start.1) | collective-permute-done | bytes 458784 | tf_op jit(solution)/shard_map/ppermute | solution.py:82
  161.0 3.6 %collective-permute-start.3 = (bf16[256,896]{1,0:T(8,128)(2,1)S(1)}, bf16[256,896]{1,0:T(8,128)(2,1)S(1)}, u32[]{:S(2)}, u32[]{:S(2)}) collective-permute-start(bf16[256,896]{1,0:T(8,128)(2,1)S(1)} %get-tuple-element.8), channel_id=1, source_target_pairs={{0,3},{1,2},{2,1},{3,0},{4,7},{5,6},{6,5},{7,4},{8,11},{9,10},{10,... | collective-permute-start | bytes 1376264 | tf_op jit(solution)/shard_map/ppermute | solution.py:82
  165.1 3.2 %fusion.8 = bf16[256,1792]{0,1:T(8,128)(2,1)S(1)} fusion(bf16[128,4,2,1792]{0,3,1,2:T(8,128)(2,1)} %all-gather.5.cloned.1.call-done, bf16[4,128,2,256]{3,0,2,1:T(4,128)(2,1)S(1)} %bitcast.87), kind=kOutput, calls=%fused_computation.9 | convolution fusion | flops 939982848 | bytes 5111808 | tf_op jit(solution)/shard_map/gsch,sgcd->hd/dot_general | solution.py:73
  168.3 1.7 convolution_convert_fusion.1
  170.0 2.5 %collective-permute-start.2 = (bf16[256,896]{0,1:T(8,128)(2,1)S(1)}, bf16[256,896]{0,1:T(8,128)(2,1)S(1)}, u32[]{:S(2)}, u32[]{:S(2)}) collective-permute-start(bf16[256,896]{0,1:T(8,128)(2,1)S(1)} %convolution_convert_fusion.1), channel_id=1, source_target_pairs={{0,1},{1,0},{2,3},{3,2},{4,5},{5,4},{6,7},{7,6},{8,9},{9,8},{10,11... | collective-permute-start | bytes 1376264 | tf_op jit(solution)/shard_map/ppermute | solution.py:89
  172.6 1.8 collective-permute-done.3
  175.0 7.6 %collective-permute-done.2 = bf16[256,896]{0,1:T(8,128)(2,1)S(1)} collective-permute-done((bf16[256,896]{0,1:T(8,128)(2,1)S(1)}, bf16[256,896]{0,1:T(8,128)(2,1)S(1)}, u32[]{:S(2)}, u32[]{:S(2)}) %collective-permute-start.2) | collective-permute-done | bytes 458784 | tf_op jit(solution)/shard_map/ppermute | solution.py:89
  182.6 3.0 %collective-permute-start.4 = (bf16[256,896]{0,1:T(8,128)(2,1)S(1)}, bf16[256,896]{0,1:T(8,128)(2,1)S(1)}, u32[]{:S(2)}, u32[]{:S(2)}) collective-permute-start(bf16[256,896]{0,1:T(8,128)(2,1)S(1)} %convolution_convert_fusion), channel_id=1, source_target_pairs={{0,1},{1,0},{2,3},{3,2},{4,5},{5,4},{6,7},{7,6},{8,9},{9,8},{10,11... | collective-permute-start | bytes 1376264 | tf_op jit(solution)/shard_map/ppermute | solution.py:89
  185.6 6.0 %fusion.15 = bf16[1,1,256,1024]{3,2,1,0:T(8,128)(2,1)} fusion(bf16[256,3584]{1,0:T(8,128)(2,1)S(1)} %copy-done, bf16[1,1024,3584]{2,1,0:T(8,128)(2,1)} %all-gather.3.cloned.1.call-done), kind=kOutput, calls=%fused_computation.20 | convolution fusion | flops 1879310336 | bytes 9699328 | tf_op jit(solution)/shard_map/rd,hd->rh/dot_general | solution.py:65
  191.6 1.7 fusion.13
  193.3 1.0 collective-permute-done.4
  194.9 2.6 %copy.59 = bf16[1,256,3584]{2,1,0:T(8,128)(2,1)} copy(bf16[1,256,3584]{1,2,0:T(8,128)(2,1)S(1)} %maximum_bitcast_fusion) | data formatting | bytes 3670016
  197.4 4.1 %reshape.106 = bf16[256,3584]{1,0:T(8,128)(2,1)S(1)} reshape(bf16[128,2,3584]{2,1,0:T(2,128)(2,1)} %all-to-all-done) | data formatting | bytes 3670016 | tf_op jit(solution)/shard_map/reshape | solution.py:49
  201.5 1.1 gather_fusion
  (58 shorter events, 9.1 us)
Async XLA Ops:
  7.2 0.8 copy-start.6
  7.2 1.1 copy-start.7
  7.2 1.8 copy-start.4
  7.2 88.9 %all-gather.3.cloned.1.call-start = ((), (), s32[]{:S(2)}) async-start(), calls=%async_computation.3 | async-start | bytes 9175040 | tf_op jit(solution)/shard_map/all_gather | solution.py:43
  7.9 157.2 %all-gather.5.cloned.1.call-start = ((), (), s32[]{:S(2)}) async-start(), calls=%async_computation.4 | async-start | bytes 4587520 | tf_op jit(solution)/shard_map/all_gather | solution.py:70
  81.7 2.3 %copy-start.1 = (bf16[1,1,256,1024]{3,2,1,0:T(8,128)(2,1)S(1)}, bf16[1,1,256,1024]{3,2,1,0:T(8,128)(2,1)}, u32[]{:S(2)}) copy-start(bf16[1,1,256,1024]{3,2,1,0:T(8,128)(2,1)} %param.5) | copy-start | bytes 1572868
  92.0 15.2 %all-to-all-start.2 = ((bf16[4,2,32768]{2,1,0:T(2,128)(2,1)}), bf16[4,2,32768]{2,1,0:T(2,128)(2,1)S(1)}, u32[]{:S(2)}, u32[]{:S(2)}) async-start(bf16[4,2,32768]{2,1,0:T(2,128)(2,1)} %reshape.136), calls=%async_computation.2 | async-start | bytes 1048576 | tf_op jit(solution)/shard_map/all_to_all | solution.py:68
  107.2 90.2 %all-to-all-start = ((bf16[128,2,3584]{2,1,0:T(2,128)(2,1)}), bf16[128,2,3584]{2,1,0:T(2,128)(2,1)}, u32[]{:S(2)}, u32[]{:S(2)}) async-start(bf16[128,2,3584]{2,1,0:T(2,128)(2,1)} %reshape.105), calls=%async_computation | async-start | bytes 3670016 | tf_op jit(solution)/shard_map/all_to_all | solution.py:46
  124.2 17.0 %collective-permute-start = (bf16[256,512]{1,0:T(8,128)(2,1)}, bf16[256,512]{1,0:T(8,128)(2,1)}, u32[]{:S(2)}, u32[]{:S(2)}) collective-permute-start(bf16[256,512]{1,0:T(8,128)(2,1)} %dynamic-slice_bitcast_fusion), channel_id=1, source_target_pairs={{0,3},{1,2},{2,1},{3,0},{4,7},{5,6},{6,5},{7,4},{8,11},{9,10},{10,... | collective-permute-start | bytes 786440 | tf_op jit(solution)/shard_map/ppermute | solution.py:36
  131.7 29.3 %collective-permute-start.1 = (bf16[256,896]{1,0:T(8,128)(2,1)}, bf16[256,896]{1,0:T(8,128)(2,1)}, u32[]{:S(2)}, u32[]{:S(2)}) collective-permute-start(bf16[256,896]{1,0:T(8,128)(2,1)} %get-tuple-element.26), channel_id=1, source_target_pairs={{0,3},{1,2},{2,1},{3,0},{4,7},{5,6},{6,5},{7,4},{8,11},{9,10},{10,... | collective-permute-start | bytes 1376264 | tf_op jit(solution)/shard_map/ppermute | solution.py:82
  161.0 13.5 %collective-permute-start.3 = (bf16[256,896]{1,0:T(8,128)(2,1)S(1)}, bf16[256,896]{1,0:T(8,128)(2,1)S(1)}, u32[]{:S(2)}, u32[]{:S(2)}) collective-permute-start(bf16[256,896]{1,0:T(8,128)(2,1)S(1)} %get-tuple-element.8), channel_id=1, source_target_pairs={{0,3},{1,2},{2,1},{3,0},{4,7},{5,6},{6,5},{7,4},{8,11},{9,10},{10,... | collective-permute-start | bytes 1376264 | tf_op jit(solution)/shard_map/ppermute | solution.py:82
  165.1 3.2 %copy-start.2 = (bf16[256,256]{1,0:T(8,128)(2,1)S(1)}, bf16[256,256]{1,0:T(8,128)(2,1)}, u32[]{:S(2)}) copy-start(bf16[256,256]{1,0:T(8,128)(2,1)} %get-tuple-element.29) | copy-start | bytes 393220
  165.1 3.2 %copy-start.3 = (bf16[256,256]{1,0:T(8,128)(2,1)S(1)}, bf16[256,256]{1,0:T(8,128)(2,1)}, u32[]{:S(2)}) copy-start(bf16[256,256]{1,0:T(8,128)(2,1)} %get-tuple-element.31) | copy-start | bytes 393220
  170.0 15.6 %copy-start = (bf16[256,3584]{1,0:T(8,128)(2,1)S(1)}, bf16[256,3584]{1,0:T(8,128)(2,1)}, u32[]{:S(2)}) copy-start(bf16[256,3584]{1,0:T(8,128)(2,1)} %reshape.109) | copy-start | bytes 5505028
  170.0 12.6 %collective-permute-start.2 = (bf16[256,896]{0,1:T(8,128)(2,1)S(1)}, bf16[256,896]{0,1:T(8,128)(2,1)S(1)}, u32[]{:S(2)}, u32[]{:S(2)}) collective-permute-start(bf16[256,896]{0,1:T(8,128)(2,1)S(1)} %convolution_convert_fusion.1), channel_id=1, source_target_pairs={{0,1},{1,0},{2,3},{3,2},{4,5},{5,4},{6,7},{7,6},{8,9},{9,8},{10,11... | collective-permute-start | bytes 1376264 | tf_op jit(solution)/shard_map/ppermute | solution.py:89
  182.6 11.6 %collective-permute-start.4 = (bf16[256,896]{0,1:T(8,128)(2,1)S(1)}, bf16[256,896]{0,1:T(8,128)(2,1)S(1)}, u32[]{:S(2)}, u32[]{:S(2)}) collective-permute-start(bf16[256,896]{0,1:T(8,128)(2,1)S(1)} %convolution_convert_fusion), channel_id=1, source_target_pairs={{0,1},{1,0},{2,3},{3,2},{4,5},{5,4},{6,7},{7,6},{8,9},{9,8},{10,11... | collective-permute-start | bytes 1376264 | tf_op jit(solution)/shard_map/ppermute | solution.py:89
  201.5 2.2 %copy-start.5 = (bf16[1,16,3584]{2,1,0:T(8,128)(2,1)S(1)}, bf16[1,16,3584]{2,1,0:T(8,128)(2,1)}, u32[]{:S(2)}) copy-start(bf16[1,16,3584]{2,1,0:T(8,128)(2,1)} %param.9) | copy-start | bytes 344068
Sparse Core Ops, SparseCore 0:
  10.1 84.9 all-gather.2
  97.2 67.8 all-gather.4

commit v6 on v0

--- a/solution.py
+++ b/solution.py
@@ -2,6 +2,7 @@
 import jax.numpy as jnp
 from jax import lax
 from jax.sharding import PartitionSpec as P
+from jax.experimental.layout import Layout, with_layout_constraint
 
 
 def slot_ranks(choices, experts):
@@ -51,6 +52,7 @@
     d_weight = jnp.einsum(
         "gsch,sgcd->hd", columns, slot_grads, preferred_element_type=jnp.float32
     ).astype(jnp.bfloat16)
+    d_weight = with_layout_constraint(d_weight, Layout(major_to_minor=(0, 1)))
     return (
         mixed.astype(jnp.bfloat16)[None],
         d_hidden.reshape(hidden.shape),

time: 198 us -> 197 us (level)
  local copies, waits for them, and re-layouts: 25.9 us -> 22.9 us
    all_gather x1, waiting for transfers between devices: 2.16 us -> 4.83 us  [on_device(): w_whole = lax.all_gather(w_down, 'dp', axis=1, tiled=True)[0]]
    all_to_all x1, local copies, waits for them, and re-layouts: 3.72 us -> 1.41 us  [on_device(): lax.all_to_all(outgoing.reshape(experts, 1, slots, width), 'expert', spli...]
    unnamed x18 -> x17, local copies, waits for them, and re-layouts: 6.64 us -> 4.87 us
where the time goes in v6:
time: 197 us
  blocking collectives  64.9 us (33%)
  waiting for transfers between devices  43.1 us (22%)
  starting transfers between devices  24.4 us (12%)
  local copies, waits for them, and re-layouts  22.9 us (12%)
  matrix products  20.3 us (10%)
  between operations  14.2 us (7%)
  other arithmetic  6.83 us (3%)
    all_to_all x1, blocking collectives, on_device(): lax.all_to_all(outgoing.reshape(experts, 1, slots, width), 'expert', spli...  64.9 us
    all_to_all x1, waiting for transfers between devices, on_device(): lax.all_to_all(out_slots.reshape(experts, slots, width), 'expert', split_...  34.8 us
    all_to_all x1, starting transfers between devices, on_device(): lax.all_to_all(out_slots.reshape(experts, slots, width), 'expert', split_...  20.3 us
    dot_general x1, matrix products, on_device(): jnp.einsum('rd,hd->rh', own_grads.reshape(-1, width), w_whole, preferred_...  6.54 us
    dot_general x1, matrix products, on_device(): jnp.einsum('gsch,sgcd->hd', columns, slot_grads, preferred_element_type=j...  6.41 us
    dot_general x1, matrix products, on_device(): jnp.dot(hidden[0, 0], w_whole, preferred_element_type=jnp.float32)  6.37 us
    unnamed x17, local copies, waits for them, and re-layouts  4.87 us
    all_gather x1, waiting for transfers between devices, on_device(): w_whole = lax.all_gather(w_down, 'dp', axis=1, tiled=True)[0]  4.83 us
  transfers between devices with their start and end apart: 4, of which 3 were waited for; matrix products, arithmetic and copies ran while one was open for 22% of the time, Pallas kernels for 0%

profile of v6, /device:TPU:1, one launch (start us, length us, event | category | flops | bytes accessed | tf_op | source)
XLA Modules:
  0.0 196.7 jit_solution(12261676486728659800)
XLA Ops:
  7.2 0.7 all-gather.3.cloned.1.call-update
  8.6 0.2 reduce_window_sum.11
  8.8 0.2 select_reduce_fusion
  9.0 2.5 %scatter_custom_fusion = bf16[256,3584]{1,0:T(8,128)(2,1)S(1)} fusion(s32[128]{0:T(128)S(1)} %fusion.30, f32[16,3584]{1,0:T(8,128)S(1)} %bitcast_convert_fusion.1, f32[128]{0:T(128)S(1)} %mul.53, bf16[]{:T(256)} %constant.7.clone.1), kind=kCustom, calls=%fused_computation.14 | custom fusion | flops 917504 | bytes 2064898 | tf_op jit(solution)/shard_map/scatter | solution.py:37
  11.5 1.6 reshape.99
  13.2 64.9 %all_to_all.25 = bf16[128,1,2,3584]{3,2,1,0:T(2,128)(2,1)S(1)} all-to-all(bf16[128,1,2,3584]{3,2,1,0:T(2,128)(2,1)} %bitcast.75), channel_id=1, replica_groups=mesh['expert'=128,'dp'=4] {'expert'}, dimensions={0} | all-to-all | bytes 3670016 | tf_op jit(solution)/shard_map/all_to_all | solution.py:38
  78.1 1.4 copy.48
  79.5 1.0 copy-done
  80.5 0.8 copy.49
  81.4 0.5 broadcast.58
  81.9 3.8 %reduce = bf16[1024,256]{1,0:T(8,128)(2,1)S(1)} reduce(bf16[1024,1,1,256]{3,2,1,0:T(2,128)(2,1)S(1)} %bitcast.77, bf16[]{:T(256)} %broadcast.58), dimensions={1,2}, to_apply=%bitcast.68.reduce_sub_computation | reduce | bytes 1048578
  85.7 0.9 reshape.125
  86.6 4.0 %all-to-all-start.2 = ((bf16[4,2,32768]{2,1,0:T(2,128)(2,1)}), bf16[4,2,32768]{2,1,0:T(2,128)(2,1)S(1)}, u32[]{:S(2)}, u32[]{:S(2)}) async-start(bf16[4,2,32768]{2,1,0:T(2,128)(2,1)} %reshape.125), calls=%async_computation.2 | async-start | bytes 1048576 | tf_op jit(solution)/shard_map/all_to_all | solution.py:50
  90.7 4.8 %all-gather.3.cloned.1.call-done = bf16[1,1024,3584]{2,1,0:T(8,128)(2,1)} async-done(((bf16[1,256,3584]{2,1,0:T(8,128)(2,1)}), bf16[1,1024,3584]{2,1,0:T(8,128)(2,1)}) %all-gather.3.cloned.1.call-update) | async-done | bytes 7340048 | tf_op jit(solution)/shard_map/all_gather | solution.py:20
  95.5 6.4 %fusion.5 = bf16[256,3584]{1,0:T(8,128)(2,1)} fusion(bf16[1,1024,3584]{2,1,0:T(8,128)(2,1)} %all-gather.3.cloned.1.call-done, bf16[1,1,256,1024]{3,2,1,0:T(8,128)(2,1)S(1)} %copy-done.1), kind=kOutput, calls=%fused_computation.8 | convolution fusion | flops 1879965696 | bytes 9699328 | tf_op jit(solution)/shard_map/dot_general | solution.py:21
  101.9 4.7 %reshape.96 = bf16[128,2,3584]{2,1,0:T(2,128)(2,1)} reshape(bf16[256,3584]{1,0:T(8,128)(2,1)} %fusion.5) | data formatting | bytes 3670016 | tf_op jit(solution)/shard_map/reshape | solution.py:25
  106.6 20.3 %all-to-all-start = ((bf16[128,2,3584]{2,1,0:T(2,128)(2,1)}), bf16[128,2,3584]{2,1,0:T(2,128)(2,1)}, u32[]{:S(2)}, u32[]{:S(2)}) async-start(bf16[128,2,3584]{2,1,0:T(2,128)(2,1)} %reshape.96), calls=%async_computation | async-start | bytes 3670016 | tf_op jit(solution)/shard_map/all_to_all | solution.py:24
  127.1 0.1 reshape.103
  127.3 0.5 reshape.126
  127.9 0.9 copy.57
  128.8 1.3 copy.50
  130.1 1.6 reshape_squeeze.6
  131.7 6.5 %fusion.13 = bf16[1,1,256,1024]{3,2,1,0:T(8,128)(2,1)} fusion(bf16[256,3584]{1,0:T(8,128)(2,1)} %reshape_squeeze.6, bf16[1,1024,3584]{2,1,0:T(8,128)(2,1)} %all-gather.3.cloned.1.call-done), kind=kOutput, calls=%fused_computation.13 | convolution fusion | flops 1879310336 | bytes 9699328 | tf_op jit(solution)/shard_map/rd,hd->rh/dot_general | solution.py:47
  138.3 34.8 %all-to-all-done = bf16[128,2,3584]{2,1,0:T(2,128)(2,1)} async-done(((bf16[128,2,3584]{2,1,0:T(2,128)(2,1)}), bf16[128,2,3584]{2,1,0:T(2,128)(2,1)}, u32[]{:S(2)}, u32[]{:S(2)}) %all-to-all-start) | async-done | bytes 1835040 | tf_op jit(solution)/shard_map/all_to_all | solution.py:24
  173.1 4.1 %reshape.97 = bf16[256,3584]{1,0:T(8,128)(2,1)S(1)} reshape(bf16[128,2,3584]{2,1,0:T(2,128)(2,1)} %all-to-all-done) | data formatting | bytes 3670016 | tf_op jit(solution)/shard_map/reshape | solution.py:27
  177.2 1.1 gather_fusion
  178.3 0.4 fusion.18
  178.7 0.7 copy.65
  179.3 0.6 fusion.20
  179.9 0.7 copy.56
  180.6 2.8 %all-gather.5.cloned.1.call-done = bf16[128,4,2,3584]{3,0,1,2:T(8,128)(2,1)} async-done(((bf16[128,1,2,3584]{3,0,1,2:T(8,128)(2,1)}), bf16[128,4,2,3584]{3,0,1,2:T(8,128)(2,1)}) %all-gather.5.cloned.1.call-update) | async-done | bytes 7340048 | tf_op jit(solution)/shard_map/all_gather | solution.py:46
  183.4 6.4 %fusion.8 = bf16[1,256,3584]{2,1,0:T(8,128)(2,1)} fusion(bf16[128,4,2,3584]{3,0,1,2:T(8,128)(2,1)} %all-gather.5.cloned.1.call-done, bf16[4,128,2,256]{3,0,2,1:T(4,128)(2,1)S(1)} %bitcast.78), kind=kOutput, calls=%fused_computation.9 | convolution fusion | flops 1879965696 | bytes 9699328 | tf_op jit(solution)/shard_map/gsch,sgcd->hd/dot_general | solution.py:52
  (29 shorter events, 1.0 us)
Async XLA Ops:
  7.2 0.8 copy-start.3
  7.2 1.1 copy-start.4
  7.2 1.8 copy-start.2
  7.2 88.3 %all-gather.3.cloned.1.call-start = ((), (), s32[]{:S(2)}) async-start(), calls=%async_computation.3 | async-start | bytes 9175040 | tf_op jit(solution)/shard_map/all_gather | solution.py:20
  7.9 175.5 %all-gather.5.cloned.1.call-start = ((), (), s32[]{:S(2)}) async-start(), calls=%async_computation.4 | async-start | bytes 9175040 | tf_op jit(solution)/shard_map/all_gather | solution.py:46
  79.5 1.0 copy-start
  85.7 9.8 %copy-start.1 = (bf16[1,1,256,1024]{3,2,1,0:T(8,128)(2,1)S(1)}, bf16[1,1,256,1024]{3,2,1,0:T(8,128)(2,1)}, u32[]{:S(2)}) copy-start(bf16[1,1,256,1024]{3,2,1,0:T(8,128)(2,1)} %param.5) | copy-start | bytes 1572868
  86.6 20.0 %all-to-all-start.2 = ((bf16[4,2,32768]{2,1,0:T(2,128)(2,1)}), bf16[4,2,32768]{2,1,0:T(2,128)(2,1)S(1)}, u32[]{:S(2)}, u32[]{:S(2)}) async-start(bf16[4,2,32768]{2,1,0:T(2,128)(2,1)} %reshape.125), calls=%async_computation.2 | async-start | bytes 1048576 | tf_op jit(solution)/shard_map/all_to_all | solution.py:50
  106.6 66.5 %all-to-all-start = ((bf16[128,2,3584]{2,1,0:T(2,128)(2,1)}), bf16[128,2,3584]{2,1,0:T(2,128)(2,1)}, u32[]{:S(2)}, u32[]{:S(2)}) async-start(bf16[128,2,3584]{2,1,0:T(2,128)(2,1)} %reshape.96), calls=%async_computation | async-start | bytes 3670016 | tf_op jit(solution)/shard_map/all_to_all | solution.py:24
Sparse Core Ops, SparseCore 0:
  10.1 85.3 all-gather.2
  97.6 85.7 all-gather.4

commit v7 on v6

--- a/solution.py
+++ b/solution.py
@@ -44,6 +44,7 @@
     )
     own_grads = mine[:, 0]
     slot_grads = lax.all_gather(mine, "dp", axis=1, tiled=True)
+    slot_grads = with_layout_constraint(slot_grads, Layout(major_to_minor=(1, 0, 2, 3)))
     d_hidden = jnp.einsum(
         "rd,hd->rh", own_grads.reshape(-1, width), w_whole, preferred_element_type=jnp.float32
     ).astype(jnp.bfloat16)

time: 197 us -> 197 us (level)
  transfers between devices with their start and end apart: 4 -> 4, of which waited for: 3 -> 3; matrix products, arithmetic and copies ran while one was open for 22% -> 21% of each run, Pallas kernels for 0% -> 0%
where the time goes in v7:
time: 197 us
  blocking collectives  64.9 us (33%)
  waiting for transfers between devices  44.9 us (23%)
  starting transfers between devices  24.4 us (12%)
  local copies, waits for them, and re-layouts  21.1 us (11%)
  matrix products  20.4 us (10%)
  between operations  14.2 us (7%)
  other arithmetic  6.83 us (3%)
    all_to_all x1, blocking collectives, on_device(): lax.all_to_all(outgoing.reshape(experts, 1, slots, width), 'expert', spli...  64.9 us
    all_to_all x1, waiting for transfers between devices, on_device(): lax.all_to_all(out_slots.reshape(experts, slots, width), 'expert', split_...  36.5 us
    all_to_all x1, starting transfers between devices, on_device(): lax.all_to_all(out_slots.reshape(experts, slots, width), 'expert', split_...  20.3 us
    dot_general x1, matrix products, on_device(): jnp.einsum('rd,hd->rh', own_grads.reshape(-1, width), w_whole, preferred_...  6.64 us
    dot_general x1, matrix products, on_device(): jnp.einsum('gsch,sgcd->hd', columns, slot_grads, preferred_element_type=j...  6.41 us
    dot_general x1, matrix products, on_device(): jnp.dot(hidden[0, 0], w_whole, preferred_element_type=jnp.float32)  6.37 us
    all_gather x1, waiting for transfers between devices, on_device(): w_whole = lax.all_gather(w_down, 'dp', axis=1, tiled=True)[0]  4.83 us
    reshape x1, local copies, waits for them, and re-layouts, on_device(): out_slots.reshape(experts, slots, width)  4.75 us
  transfers between devices with their start and end apart: 4, of which 3 were waited for; matrix products, arithmetic and copies ran while one was open for 21% of the time, Pallas kernels for 0%

profile of v7, /device:TPU:1, one launch (start us, length us, event | category | flops | bytes accessed | tf_op | source)
XLA Modules:
  0.0 196.7 jit_solution(17713640946967735479)
XLA Ops:
  7.2 0.7 all-gather.3.cloned.1.call-update
  8.1 0.1 eq.15
  8.6 0.2 reduce_window_sum.11
  8.8 0.2 select_reduce_fusion
  9.0 2.5 %scatter_custom_fusion = bf16[256,3584]{1,0:T(8,128)(2,1)S(1)} fusion(s32[128]{0:T(128)S(1)} %fusion.39, f32[16,3584]{1,0:T(8,128)S(1)} %bitcast_convert_fusion.1, f32[128]{0:T(128)S(1)} %mul.53, bf16[]{:T(256)} %constant.7.clone.1), kind=kCustom, calls=%fused_computation.16 | custom fusion | flops 917504 | bytes 2064898 | tf_op jit(solution)/shard_map/scatter | solution.py:37
  11.5 1.6 reshape.99
  13.2 64.9 %all_to_all.25 = bf16[128,1,2,3584]{3,2,1,0:T(2,128)(2,1)S(1)} all-to-all(bf16[128,1,2,3584]{3,2,1,0:T(2,128)(2,1)} %reshape.99), channel_id=1, replica_groups=mesh['expert'=128,'dp'=4] {'expert'}, dimensions={0} | all-to-all | bytes 3670016 | tf_op jit(solution)/shard_map/all_to_all | solution.py:38
  78.1 1.4 copy.38
  79.5 1.0 copy-done
  80.5 0.8 copy.40
  81.4 0.5 broadcast.58
  81.9 3.8 %reduce = bf16[1024,256]{1,0:T(8,128)(2,1)S(1)} reduce(bf16[1024,1,1,256]{3,2,1,0:T(2,128)(2,1)S(1)} %bitcast.74, bf16[]{:T(256)} %broadcast.58), dimensions={1,2}, to_apply=%bitcast.67.reduce_sub_computation | reduce | bytes 1048578
  85.7 0.9 reshape.125
  86.6 4.0 %all-to-all-start.2 = ((bf16[4,2,32768]{2,1,0:T(2,128)(2,1)}), bf16[4,2,32768]{2,1,0:T(2,128)(2,1)S(1)}, u32[]{:S(2)}, u32[]{:S(2)}) async-start(bf16[4,2,32768]{2,1,0:T(2,128)(2,1)} %reshape.125), calls=%async_computation.2 | async-start | bytes 1048576 | tf_op jit(solution)/shard_map/all_to_all | solution.py:51
  90.7 4.8 %all-gather.3.cloned.1.call-done = bf16[1,1024,3584]{2,1,0:T(8,128)(2,1)} async-done(((bf16[1,256,3584]{2,1,0:T(8,128)(2,1)}), bf16[1,1024,3584]{2,1,0:T(8,128)(2,1)}) %all-gather.3.cloned.1.call-update) | async-done | bytes 7340048 | tf_op jit(solution)/shard_map/all_gather | solution.py:20
  95.5 6.4 %fusion.12 = bf16[256,3584]{1,0:T(8,128)(2,1)} fusion(bf16[1,1024,3584]{2,1,0:T(8,128)(2,1)} %all-gather.3.cloned.1.call-done, bf16[1,1,256,1024]{3,2,1,0:T(8,128)(2,1)S(1)} %copy-done.1), kind=kOutput, calls=%fused_computation.10 | convolution fusion | flops 1879965696 | bytes 9699328 | tf_op jit(solution)/shard_map/dot_general | solution.py:21
  101.9 4.7 %reshape.96 = bf16[128,2,3584]{2,1,0:T(2,128)(2,1)} reshape(bf16[256,3584]{1,0:T(8,128)(2,1)} %fusion.12) | data formatting | bytes 3670016 | tf_op jit(solution)/shard_map/reshape | solution.py:25
  106.6 20.3 %all-to-all-start = ((bf16[128,2,3584]{2,1,0:T(2,128)(2,1)}), bf16[128,2,3584]{2,1,0:T(2,128)(2,1)}, u32[]{:S(2)}, u32[]{:S(2)}) async-start(bf16[128,2,3584]{2,1,0:T(2,128)(2,1)} %reshape.96), calls=%async_computation | async-start | bytes 3670016 | tf_op jit(solution)/shard_map/all_to_all | solution.py:24
  127.1 0.1 reshape.103
  127.3 0.5 reshape.126
  128.0 0.3 copy.41
  128.3 1.6 reshape_squeeze.6
  129.9 6.6 %fusion.22 = bf16[1,1,256,1024]{3,2,1,0:T(8,128)(2,1)} fusion(bf16[256,3584]{1,0:T(8,128)(2,1)} %reshape_squeeze.6, bf16[1,1024,3584]{2,1,0:T(8,128)(2,1)} %all-gather.3.cloned.1.call-done), kind=kOutput, calls=%fused_computation.15 | convolution fusion | flops 1879310336 | bytes 9699328 | tf_op jit(solution)/shard_map/rd,hd->rh/dot_general | solution.py:48
  136.6 36.5 %all-to-all-done = bf16[128,2,3584]{2,1,0:T(2,128)(2,1)} async-done(((bf16[128,2,3584]{2,1,0:T(2,128)(2,1)}), bf16[128,2,3584]{2,1,0:T(2,128)(2,1)}, u32[]{:S(2)}, u32[]{:S(2)}) %all-to-all-start) | async-done | bytes 1835040 | tf_op jit(solution)/shard_map/all_to_all | solution.py:24
  173.1 4.1 %reshape.97 = bf16[256,3584]{1,0:T(8,128)(2,1)S(1)} reshape(bf16[128,2,3584]{2,1,0:T(2,128)(2,1)} %all-to-all-done) | data formatting | bytes 3670016 | tf_op jit(solution)/shard_map/reshape | solution.py:27
  177.2 1.1 gather_fusion
  178.3 0.4 fusion.27
  178.7 0.7 copy.66
  179.3 0.6 fusion.29
  179.9 0.7 copy.48
  180.6 2.8 %all-gather.5.cloned.1.call-done = bf16[128,4,2,3584]{3,0,2,1:T(8,128)(2,1)} async-done(((bf16[128,1,2,3584]{3,0,2,1:T(8,128)(2,1)}), bf16[128,4,2,3584]{3,0,2,1:T(8,128)(2,1)}) %all-gather.5.cloned.1.call-update) | async-done | bytes 7340048 | tf_op jit(solution)/shard_map/all_gather | solution.py:46
  183.4 6.4 %fusion.15 = bf16[1,256,3584]{2,1,0:T(8,128)(2,1)} fusion(bf16[128,4,2,3584]{3,0,2,1:T(8,128)(2,1)} %all-gather.5.cloned.1.call-done, bf16[4,128,2,256]{3,0,2,1:T(4,128)(2,1)S(1)} %bitcast.76), kind=kOutput, calls=%fused_computation.11 | convolution fusion | flops 1879965696 | bytes 9699328 | tf_op jit(solution)/shard_map/gsch,sgcd->hd/dot_general | solution.py:53
  (29 shorter events, 1.0 us)
Async XLA Ops:
  7.2 0.8 copy-start.3
  7.2 1.1 copy-start.4
  7.2 1.8 copy-start.2
  7.2 88.3 %all-gather.3.cloned.1.call-start = ((), (), s32[]{:S(2)}) async-start(), calls=%async_computation.3 | async-start | bytes 9175040 | tf_op jit(solution)/shard_map/all_gather | solution.py:20
  7.9 175.5 %all-gather.5.cloned.1.call-start = ((), (), s32[]{:S(2)}) async-start(), calls=%async_computation.4 | async-start | bytes 9175040 | tf_op jit(solution)/shard_map/all_gather | solution.py:46
  79.5 1.0 copy-start
  85.7 9.8 %copy-start.1 = (bf16[1,1,256,1024]{3,2,1,0:T(8,128)(2,1)S(1)}, bf16[1,1,256,1024]{3,2,1,0:T(8,128)(2,1)}, u32[]{:S(2)}) copy-start(bf16[1,1,256,1024]{3,2,1,0:T(8,128)(2,1)} %param.5) | copy-start | bytes 1572868
  86.6 20.0 %all-to-all-start.2 = ((bf16[4,2,32768]{2,1,0:T(2,128)(2,1)}), bf16[4,2,32768]{2,1,0:T(2,128)(2,1)S(1)}, u32[]{:S(2)}, u32[]{:S(2)}) async-start(bf16[4,2,32768]{2,1,0:T(2,128)(2,1)} %reshape.125), calls=%async_computation.2 | async-start | bytes 1048576 | tf_op jit(solution)/shard_map/all_to_all | solution.py:51
  106.6 66.5 %all-to-all-start = ((bf16[128,2,3584]{2,1,0:T(2,128)(2,1)}), bf16[128,2,3584]{2,1,0:T(2,128)(2,1)}, u32[]{:S(2)}, u32[]{:S(2)}) async-start(bf16[128,2,3584]{2,1,0:T(2,128)(2,1)} %reshape.96), calls=%async_computation | async-start | bytes 3670016 | tf_op jit(solution)/shard_map/all_to_all | solution.py:24
Sparse Core Ops, SparseCore 0:
  10.1 85.3 all-gather.2
  97.6 85.7 all-gather.4
